TPU v7x, 32 devices: a whole 2x2x4 slice. The times are simulated.
32 devices in a mesh: actors: 8 (over z, y), rep: 4 (over x, core).
Axes of the slice: x: 2, y: 2, z: 4, core: 2. Of those that a mesh axis runs over, the one named last changes fastest.
Arguments:
- features: bfloat16 [4, 8, 16, 1024], P('rep', 'actors'), may hold values from -6 to 6
- rewards: float32 [4, 8, 16], P('rep', 'actors'), may hold values from -2 to 6, as said below
- lengths: int32 [4, 8, 8], P('rep', 'actors'), may hold values from 1 to 3, 16 in all within a row
- owners: int32 [4, 8, 8], P('rep', 'actors'), may hold values from 0 to 7, each once within a row
- norm_gain: float32 [1024], replicated, may hold values from 0.4 to 1.6
Outputs:
- trainer_rows: bfloat16 [4, 8, 24, 1024], P('rep', 'actors')
- trainer_rewards: float32 [4, 8, 24], P('rep', 'actors')
- trainer_counts: int32 [8], P('actors')
Inputs may be any that keep to these rules, and one draw needn't show every extreme that they name: `rewards`: rewards of each actor are centered on a level that differs from actor to actor.
All inputs are finite; a program needn't handle non-finite values.
Results may differ from a plain program's by a relative error of at most 0.0004.
Values may be sent and summed in bfloat16 or wider, within the bound.
No kernel may reach another device: no remote copies, remote signals or barrier semaphores. Data moves between devices by JAX's collectives and lax.ppermute only.
A program may use at most 64 MiB of HBM per device.

v0:
```python
import jax
import jax.numpy as jnp
from jax import lax
from jax.sharding import PartitionSpec as P

CAP = 3


EPS_NORM = 1e-06
EPS_VAR = 1e-05


def rms_scale(rows, norm_gain):
    widened = rows.astype(jnp.float32)
    square_mean = jnp.mean(widened * widened, axis=-1, keepdims=True)
    return (widened * lax.rsqrt(square_mean + EPS_NORM) * norm_gain).astype(jnp.bfloat16)


def local(features, rewards, lengths, owners, norm_gain):
    rows_here = features[0, 0]
    reward_here = rewards[0, 0]
    game_len = lengths[0, 0]
    game_owner = owners[0, 0]
    games = game_len.shape[0]
    row_count = rows_here.shape[0]
    width = rows_here.shape[1]
    row_total = row_count * lax.axis_size("actors") * lax.axis_size("rep")
    starts = jnp.cumsum(game_len) - game_len
    trainer_ids = jnp.arange(games, dtype=jnp.int32)
    owns_game = (game_owner[None, :] == trainer_ids[:, None]).astype(jnp.int32)
    held_len = jnp.sum(owns_game * game_len[None, :], axis=1)
    held_start = jnp.sum(owns_game * starts[None, :], axis=1)
    slot_pos = jnp.arange(CAP, dtype=jnp.int32)
    usable = slot_pos[None, :] < held_len[:, None]
    row_index = jnp.minimum(held_start[:, None] + slot_pos[None, :], row_count - 1)
    outgoing = jnp.where(
        usable, jnp.take(reward_here, row_index, axis=0), jnp.zeros((), jnp.float32)
    )
    arrived, arrived_len = (
        lax.all_to_all(outgoing, "actors", split_axis=0, concat_axis=0, tiled=True),
        lax.all_to_all(
            held_len.astype(jnp.float32)[:, None], "actors", split_axis=0, concat_axis=0, tiled=True
        ),
    )
    normed = rms_scale(rows_here, norm_gain)
    packed = jnp.where(
        usable[:, :, None], jnp.take(normed, row_index, axis=0), jnp.zeros((), jnp.bfloat16)
    )
    landed = lax.all_to_all(packed, "actors", split_axis=0, concat_axis=0, tiled=True)
    first, second = lax.psum((jnp.sum(arrived), jnp.sum(arrived * arrived)), ("actors", "rep"))
    reward_mean = first / row_total
    inv_spread = lax.rsqrt(second / row_total - reward_mean * reward_mean + EPS_VAR)
    keep_slot = slot_pos[None, :].astype(jnp.float32) < arrived_len
    scaled = jnp.where(keep_slot, (arrived - reward_mean) * inv_spread, jnp.zeros((), jnp.float32))
    count_here = jnp.sum(arrived_len).astype(jnp.int32)
    counts = lax.psum(count_here, "rep")
    return (landed.reshape(1, 1, -1, width), scaled.reshape(1, 1, -1), counts.reshape(1))


def solution(mesh):
    return jax.shard_map(
        local,
        mesh=mesh,
        in_specs=(
            P("rep", "actors", None, None),
            P("rep", "actors", None),
            P("rep", "actors", None),
            P("rep", "actors", None),
            P(),
        ),
        out_specs=(P("rep", "actors", None, None), P("rep", "actors", None), P("actors")),
        check_vma=False,
    )
```

profile of v0, /device:TPU:0, one launch (start us, length us, event | category | flops | bytes accessed | tf_op | source)
XLA Modules:
  0.0 78.4 jit_solution(11744744199554701349)
XLA Ops:
  0.6 0.0 copy-start
  0.6 0.0 copy-start.3
  0.7 0.6 copy-done.3
  1.3 0.2 reduce-window.8
  1.5 0.8 %select_reduce_fusion.1 = (s32[8]{0:T(128)S(1)}, s32[8]{0:T(128)S(1)}) fusion(s32[8]{0:T(128)S(1)} %bitcast.19, s32[8]{0:T(128)} %bitcast.20, s32[8]{0:T(128)S(1)} %bitcast_subtract_fusion), kind=kLoop, calls=%fused_computation.21 | loop fusion | flops 304 | bytes 160 | tf_op jit(solution)/shard_map/reduce_sum | solution.py:31
  2.3 0.7 copy.12
  3.0 7.3 %all-to-all-start.1 = ((f32[8,1,1]{2,1,0:T(1,128)}), f32[8,1,1]{2,1,0:T(1,128)S(1)}, u32[]{:S(2)}, u32[]{:S(2)}) async-start(f32[8,1,1]{2,1,0:T(1,128)} %copy.12), calls=%async_computation.1 | async-start | bytes 8192 | tf_op jit(solution)/shard_map/all_to_all | solution.py:41
  10.3 0.1 iota_compare_fusion.2
  10.4 0.1 compare_select_fusion.1
  10.4 0.1 fusion
  10.6 0.1 reshape.286
  10.7 0.7 gather_fusion.1
  11.4 0.1 gather.12
  11.5 0.7 select_select_fusion.1
  12.1 0.0 copy-done.2
  12.2 0.1 fusion.2
  12.2 0.6 gather_fusion
  12.9 0.7 select_select_fusion
  13.6 3.1 %all-to-all-done.1 = f32[8,1,1]{2,1,0:T(1,128)S(1)} async-done(((f32[8,1,1]{2,1,0:T(1,128)}), f32[8,1,1]{2,1,0:T(1,128)S(1)}, u32[]{:S(2)}, u32[]{:S(2)}) %all-to-all-start.1) | async-done | bytes 64 | tf_op jit(solution)/shard_map/all_to_all | solution.py:41
  16.7 3.3 %all-to-all-start.2 = ((f32[8,1,3]{2,1,0:T(1,128)}), f32[8,1,3]{2,1,0:T(1,128)S(1)}, u32[]{:S(2)}, u32[]{:S(2)}) async-start(f32[8,1,3]{2,1,0:T(1,128)} %bitcast.8), calls=%async_computation.2 | async-start | bytes 8192 | tf_op jit(solution)/shard_map/all_to_all | solution.py:40
  20.0 0.6 fusion.9
  21.3 0.1 broadcast_compare_fusion
  21.3 6.1 %psum.23 = s32[1]{0:T(128)} all-reduce(s32[1]{0:T(128)} %bitcast.9), channel_id=1, replica_groups=mesh['actors'=8,'rep'=4] {'rep'}, use_global_device_ids=true, to_apply=%region_9.10 | all-reduce | flops 1 | bytes 8 | tf_op jit(solution)/shard_map/psum | solution.py:56
  27.5 0.1 lt.98
  27.6 0.0 all-to-all-done.2
  27.6 5.9 %all-to-all-start = ((bf16[8,3,1024]{2,1,0:T(4,128)(2,1)}), bf16[8,3,1024]{2,1,0:T(4,128)(2,1)S(1)}, u32[]{:S(2)}, u32[]{:S(2)}) async-start(bf16[8,3,1024]{2,1,0:T(4,128)(2,1)} %select_select_fusion), calls=%async_computation | async-start | bytes 131072 | tf_op jit(solution)/shard_map/all_to_all | solution.py:49
  33.5 0.6 fusion.10
  34.1 40.3 %all-reduce = (f32[]{:T(128)}, f32[]{:T(128)}) all-reduce(f32[]{:T(128)} %get-tuple-element.6, f32[]{:T(128)} %get-tuple-element.5), channel_id=1, replica_groups=mesh['actors'=8,'rep'=4] {'actors','rep'}, use_global_device_ids=true, to_apply=%region_7.8 | all-reduce | flops 2 | bytes 16 | tf_op jit(solution)/shard_map/psum | solution.py:50
  77.1 0.1 mul.77
  77.2 0.5 broadcast_select_fusion
  77.7 0.0 all-to-all-done
  77.7 0.7 reshape.281
  (11 shorter events, 0.1 us)
Async XLA Ops:
  0.6 10.0 %copy-start = (f32[1,1,16]{2,1,0:T(1,128)S(1)}, f32[1,1,16]{2,1,0:T(1,128)}, u32[]{:S(2)}) copy-start(f32[1,1,16]{2,1,0:T(1,128)} %param.6) | copy-start | bytes 196
  0.6 0.7 copy-start.3
  0.7 9.8 %copy-start.1 = (bf16[1,1,16,1024]{3,2,1,0:T(8,128)(2,1)S(1)}, bf16[1,1,16,1024]{3,2,1,0:T(8,128)(2,1)}, u32[]{:S(2)}) copy-start(bf16[1,1,16,1024]{3,2,1,0:T(8,128)(2,1)} %param.5) | copy-start | bytes 98308
  3.0 13.7 %all-to-all-start.1 = ((f32[8,1,1]{2,1,0:T(1,128)}), f32[8,1,1]{2,1,0:T(1,128)S(1)}, u32[]{:S(2)}, u32[]{:S(2)}) async-start(f32[8,1,1]{2,1,0:T(1,128)} %copy.12), calls=%async_computation.1 | async-start | bytes 8192 | tf_op jit(solution)/shard_map/all_to_all | solution.py:41
  11.5 0.7 copy-start.2
  16.7 10.9 %all-to-all-start.2 = ((f32[8,1,3]{2,1,0:T(1,128)}), f32[8,1,3]{2,1,0:T(1,128)S(1)}, u32[]{:S(2)}, u32[]{:S(2)}) async-start(f32[8,1,3]{2,1,0:T(1,128)} %bitcast.8), calls=%async_computation.2 | async-start | bytes 8192 | tf_op jit(solution)/shard_map/all_to_all | solution.py:40
  27.6 50.1 %all-to-all-start = ((bf16[8,3,1024]{2,1,0:T(4,128)(2,1)}), bf16[8,3,1024]{2,1,0:T(4,128)(2,1)S(1)}, u32[]{:S(2)}, u32[]{:S(2)}) async-start(bf16[8,3,1024]{2,1,0:T(4,128)(2,1)} %select_select_fusion), calls=%async_computation | async-start | bytes 131072 | tf_op jit(solution)/shard_map/all_to_all | solution.py:49
where the time goes:
time: 79 us; the launch traced here: 78.4 us
  blocking collectives  46.4 us (59%)
  starting transfers between devices  16.5 us (21%)
  other arithmetic  4.59 us (6%)
  between operations  4 us (5%)
  local copies, waits for them, and re-layouts  3.69 us (5%)
  waiting for transfers between devices  3.1 us (4%)
    psum x1, blocking collectives, local(): lax.psum((jnp.sum(arrived), jnp.sum(arrived * arrived)), ('actors', 'rep'))  40.3 us
    all_to_all x1, starting transfers between devices, local(): lax.all_to_all(held_len.astype(jnp.float32)[:, None], 'actors', split_axi...  7.31 us
    psum x1, blocking collectives, local(): counts = lax.psum(count_here, 'rep')  6.13 us
    all_to_all x1, starting transfers between devices, local(): lax.all_to_all(packed, 'actors', split_axis=0, concat_axis=0, tiled=True)  5.94 us
    all_to_all x1, starting transfers between devices, local(): lax.all_to_all(outgoing, 'actors', split_axis=0, concat_axis=0, tiled=True)  3.29 us
    all_to_all x1, waiting for transfers between devices, local(): lax.all_to_all(held_len.astype(jnp.float32)[:, None], 'actors', split_axi...  3.09 us
  transfers between devices with their start and end apart: 3, of which 1 were waited for; matrix products, arithmetic and copies ran while one was open for 7% of the time, Pallas kernels for 0%

commit v1 on v0

--- a/solution.py
+++ b/solution.py
@@ -1,13 +1,155 @@
+import functools
+
 import jax
 import jax.numpy as jnp
 from jax import lax
+from jax.experimental import pallas as pl
+from jax.experimental.pallas import tpu as pltpu
 from jax.sharding import PartitionSpec as P
 
 CAP = 3
-
-
 EPS_NORM = 1e-06
 EPS_VAR = 1e-05
+
+LANES = 128
+LEN_AT, SUM_AT, SQUARE_AT = CAP, CAP + 1, CAP + 2
+BLOCK = 8
+SCALARS = 2 * CAP
+
+
+def pack_kernel(groups, length_ref, owner_ref, rows_ref, gain_ref, reward_ref, out_ref, start_of, length_of):
+    games = length_ref.shape[1]
+    row_count, width = rows_ref.shape
+    half = width // 2
+    mine = lax.axis_index("rep")
+
+    start = jnp.int32(0)
+    for game in range(games):
+        size = length_ref[0, game]
+        owner = owner_ref[0, game]
+        start_of[owner] = start
+        length_of[owner] = size
+        start = start + size
+
+    padded = -(-games // 16) * 16
+    trainer = lax.broadcasted_iota(jnp.int32, (padded, LANES), 0)
+    lane = lax.broadcasted_iota(jnp.int32, (padded, LANES), 1)
+    first = jnp.zeros((padded, LANES), jnp.int32)
+    size = jnp.zeros((padded, LANES), jnp.int32)
+    for t in range(games):
+        first = jnp.where(trainer == t, start_of[t], first)
+        size = jnp.where(trainer == t, length_of[t], size)
+    reward = reward_ref[...]
+    spread = jnp.broadcast_to(reward, (padded, row_count))
+    at = lax.broadcasted_iota(jnp.int32, (padded, row_count), 1)
+    values = jnp.where(lane == LEN_AT, size.astype(jnp.float32), 0.0)
+    values = jnp.where(lane == SUM_AT, jnp.sum(reward, axis=1, keepdims=True), values)
+    values = jnp.where(lane == SQUARE_AT, jnp.sum(reward * reward, axis=1, keepdims=True), values)
+    for j in range(CAP):
+        here = (at == first[:, :row_count] + j) & (size[:, :row_count] > j)
+        values = jnp.where(lane == j, jnp.sum(jnp.where(here, spread, 0.0), axis=1, keepdims=True), values)
+    high = values.astype(jnp.bfloat16)
+    rest = values - high.astype(jnp.float32)
+    middle = rest.astype(jnp.bfloat16)
+    low = (rest - middle.astype(jnp.float32)).astype(jnp.bfloat16)
+    scalars = jnp.concatenate(
+        [high, middle, low, jnp.zeros((padded, half - 3 * LANES), jnp.bfloat16)], axis=1
+    )
+
+    wide = rows_ref[...].astype(jnp.float32)
+    square_mean = jnp.sum(wide * wide, axis=1, keepdims=True) / width
+    normed = (wide * lax.rsqrt(square_mean + EPS_NORM) * gain_ref[...]).astype(jnp.bfloat16)
+    source = jnp.concatenate([normed[:, :half], normed[:, half:], scalars], axis=0)
+
+    depth = 2 * row_count + padded
+    chunk = groups * BLOCK
+    i = lax.broadcasted_iota(jnp.int32, (chunk, depth), 0)
+    column = lax.broadcasted_iota(jnp.int32, (chunk, depth), 1)
+    group, q = i // BLOCK, i % BLOCK
+    j = q // 2
+    held = (q < SCALARS) & (group == mine)
+    offset = j + (q % 2) * row_count
+    limit = jnp.where(held, j, row_count)
+    for t in range(games):
+        wanted = jnp.where(limit < length_of[t], offset + start_of[t], -1)
+        wanted = jnp.where(q == SCALARS, 2 * row_count + t, wanted)
+        pick = jnp.where(column == wanted, 1.0, 0.0).astype(jnp.bfloat16)
+        out_ref[t * chunk : (t + 1) * chunk, :] = jnp.dot(
+            pick, source, preferred_element_type=jnp.float32
+        ).astype(jnp.bfloat16)
+
+
+def unpack_kernel(groups, rows_total, in_ref, rows_ref, reward_ref, count_ref):
+    depth, half = in_ref.shape
+    slots = rows_ref.shape[0]
+    actors = slots // CAP
+    mine = lax.axis_index("rep")
+    blocks = in_ref[...]
+
+    slot = lax.broadcasted_iota(jnp.int32, (slots, depth), 0)
+    column = lax.broadcasted_iota(jnp.int32, (slots, depth), 1)
+    at = ((slot // CAP) * groups + mine) * BLOCK + 2 * (slot % CAP)
+    left = jnp.where(column == at, 1.0, 0.0)
+    right = jnp.where(column == at + 1, 1.0, 0.0)
+    source = lax.broadcasted_iota(jnp.int32, (actors, depth), 0)
+    column = lax.broadcasted_iota(jnp.int32, (actors, depth), 1)
+    own = jnp.where(column == (source * groups + mine) * BLOCK + SCALARS, 1.0, 0.0)
+    every = jnp.where(column % BLOCK == SCALARS, 1.0, 0.0)
+    pick = jnp.concatenate([left, right, own, every], axis=0).astype(jnp.bfloat16)
+    got = jnp.dot(pick, blocks, preferred_element_type=jnp.float32)
+
+    rows_ref[:, :half] = got[:slots].astype(jnp.bfloat16)
+    rows_ref[:, half:] = got[slots : 2 * slots].astype(jnp.bfloat16)
+    scalars = got[2 * slots :, :LANES] + got[2 * slots :, LANES : 2 * LANES] + got[2 * slots :, 2 * LANES : 3 * LANES]
+    own, every = scalars[:actors], scalars[actors : 2 * actors]
+    mean = every[:, SUM_AT : SUM_AT + 1] / rows_total
+    second = every[:, SQUARE_AT : SQUARE_AT + 1] / rows_total
+    scale = lax.rsqrt(second - mean * mean + EPS_VAR)
+    lane = lax.broadcasted_iota(jnp.int32, (actors, LANES), 1)
+    source = lax.broadcasted_iota(jnp.int32, (actors, LANES), 0)
+    size = own[:, LEN_AT : LEN_AT + 1]
+    placed = jnp.zeros((actors, LANES), jnp.float32)
+    for j in range(CAP):
+        value = jnp.where(size > j, (own[:, j : j + 1] - mean) * scale, 0.0)
+        placed = jnp.where(lane == source * CAP + j, value, placed)
+    reward_ref[...] = jnp.sum(placed, axis=0, keepdims=True)[:, :slots]
+    count_ref[...] = every[:1, LEN_AT : LEN_AT + 1].astype(jnp.int32)
+
+
+def fused(features, rewards, lengths, owners, norm_gain):
+    row_count, width = features.shape[2:]
+    games = lengths.shape[2]
+    actors, groups = lax.axis_size("actors"), lax.axis_size("rep")
+    half = width // 2
+    vmem = pl.BlockSpec(memory_space=pltpu.VMEM)
+    smem = pl.BlockSpec(memory_space=pltpu.SMEM)
+    packed = pl.pallas_call(
+        functools.partial(pack_kernel, groups),
+        out_shape=jax.ShapeDtypeStruct((games * groups * BLOCK, half), jnp.bfloat16),
+        in_specs=[smem, smem, vmem, vmem, vmem],
+        out_specs=vmem,
+        scratch_shapes=[pltpu.SMEM((games,), jnp.int32), pltpu.SMEM((games,), jnp.int32)],
+        name="pack",
+    )(
+        lengths.reshape(1, games),
+        owners.reshape(1, games),
+        features.reshape(row_count, width),
+        norm_gain.reshape(1, width),
+        rewards.reshape(1, row_count),
+    )
+    landed = lax.all_to_all(packed, ("actors", "rep"), split_axis=0, concat_axis=0, tiled=True)
+    rows, scaled, count = pl.pallas_call(
+        functools.partial(unpack_kernel, groups, row_count * actors * groups),
+        out_shape=(
+            jax.ShapeDtypeStruct((actors * CAP, width), jnp.bfloat16),
+            jax.ShapeDtypeStruct((1, actors * CAP), jnp.float32),
+            jax.ShapeDtypeStruct((1, 1), jnp.int32),
+        ),
+        in_specs=[vmem],
+        out_specs=(vmem, vmem, vmem),
+        name="unpack",
+    )(landed)
+    return (rows.reshape(1, 1, -1, width), scaled.reshape(1, 1, -1), count.reshape(1))
 
 
 def rms_scale(rows, norm_gain):
@@ -16,7 +158,7 @@
     return (widened * lax.rsqrt(square_mean + EPS_NORM) * norm_gain).astype(jnp.bfloat16)
 
 
-def local(features, rewards, lengths, owners, norm_gain):
+def plain(features, rewards, lengths, owners, norm_gain):
     rows_here = features[0, 0]
     reward_here = rewards[0, 0]
     game_len = lengths[0, 0]
@@ -33,19 +175,12 @@
     slot_pos = jnp.arange(CAP, dtype=jnp.int32)
     usable = slot_pos[None, :] < held_len[:, None]
     row_index = jnp.minimum(held_start[:, None] + slot_pos[None, :], row_count - 1)
-    outgoing = jnp.where(
-        usable, jnp.take(reward_here, row_index, axis=0), jnp.zeros((), jnp.float32)
-    )
-    arrived, arrived_len = (
-        lax.all_to_all(outgoing, "actors", split_axis=0, concat_axis=0, tiled=True),
-        lax.all_to_all(
-            held_len.astype(jnp.float32)[:, None], "actors", split_axis=0, concat_axis=0, tiled=True
-        ),
-    )
+    outgoing = jnp.where(usable, jnp.take(reward_here, row_index, axis=0), jnp.zeros((), jnp.float32))
+    outgoing = jnp.concatenate([outgoing, held_len.astype(jnp.float32)[:, None]], axis=1)
+    arrived = lax.all_to_all(outgoing, "actors", split_axis=0, concat_axis=0, tiled=True)
+    arrived, arrived_len = arrived[:, :CAP], arrived[:, CAP:]
     normed = rms_scale(rows_here, norm_gain)
-    packed = jnp.where(
-        usable[:, :, None], jnp.take(normed, row_index, axis=0), jnp.zeros((), jnp.bfloat16)
-    )
+    packed = jnp.where(usable[:, :, None], jnp.take(normed, row_index, axis=0), jnp.zeros((), jnp.bfloat16))
     landed = lax.all_to_all(packed, "actors", split_axis=0, concat_axis=0, tiled=True)
     first, second = lax.psum((jnp.sum(arrived), jnp.sum(arrived * arrived)), ("actors", "rep"))
     reward_mean = first / row_total
@@ -55,6 +190,14 @@
     count_here = jnp.sum(arrived_len).astype(jnp.int32)
     counts = lax.psum(count_here, "rep")
     return (landed.reshape(1, 1, -1, width), scaled.reshape(1, 1, -1), counts.reshape(1))
+
+
+def local(features, rewards, lengths, owners, norm_gain):
+    actors, groups = lax.axis_size("actors"), lax.axis_size("rep")
+    width = features.shape[3]
+    fits = actors * CAP <= LANES and actors % 8 == 0 and width % 1024 == 0 and features.shape[2] % 16 == 0
+    step = fused if fits else plain
+    return step(features, rewards, lengths, owners, norm_gain)
 
 
 def solution(mesh):

time: 79 us -> 22.7 us (0.29)
  blocking collectives: 46.4 us -> 18 us
  starting transfers between devices: 16.5 us -> 0 us
  other arithmetic: 4.59 us -> 0 us
  Pallas kernels: 0 us -> 3.75 us
  local copies, waits for them, and re-layouts: 3.69 us -> 0 us
  between operations: 4 us -> 0.63 us
  waiting for transfers between devices: 3.1 us -> 0 us
    psum x2 -> x0, blocking collectives: 46.4 us -> none  [the longest x1 40.3 us: local(): lax.psum((jnp.sum(arrived), jnp.sum(arrived * arrived)), ('actors', 'rep'))]
    all_to_all x0 -> x1, blocking collectives: none -> 18 us  [fused(): lax.all_to_all(packed, ('actors', 'rep'), split_axis=0, concat_axis=0, ti...]
    all_to_all x3 -> x0, starting transfers between devices: 16.5 us -> none  [the longest x1 7.31 us: local(): lax.all_to_all(held_len.astype(jnp.float32)[:, None], 'actors', split_axi...]
    pallas_call x0 -> x2, Pallas kernels: none -> 3.75 us  [the longest x1 1.93 us: fused(): pl.pallas_call(functools.partial(unpack_kernel, groups, row_count * actor...]
    all_to_all x3 -> x0, waiting for transfers between devices: 3.1 us -> none  [the longest x1 3.09 us: local(): lax.all_to_all(held_len.astype(jnp.float32)[:, None], 'actors', split_axi...]
    reduce_sum x4 -> x0, other arithmetic: 2.14 us -> none  [the longest x1 0.8 us: local(): held_len = jnp.sum(owns_game * game_len[None, :], axis=1)]
    select_n x4 -> x0, other arithmetic: 1.99 us -> none  [the longest x1 0.73 us: local(): jnp.where(usable[:, :, None], jnp.take(normed, row_index, axis=0), jnp.ze...]
    gather x4 -> x0, local copies, waits for them, and re-layouts: 1.42 us -> none  [the longest x2 0.78 us: local(): jnp.take(reward_here, row_index, axis=0)]
  transfers between devices with their start and end apart: 3 -> 0, of which waited for: 1 -> 0; matrix products, arithmetic and copies ran while one was open for 7% -> 0% of each run, Pallas kernels for 0% -> 0%
where the time goes in v1:
time: 22.7 us; the launch traced here: 22.4 us
  blocking collectives  18 us (79%)
  Pallas kernels  3.75 us (17%)
  between operations  0.63 us (3%)
    all_to_all x1, blocking collectives, fused(): lax.all_to_all(packed, ('actors', 'rep'), split_axis=0, concat_axis=0, ti...  18 us
    pallas_call x1, Pallas kernels, fused(): pl.pallas_call(functools.partial(unpack_kernel, groups, row_count * actor...  1.93 us
    pallas_call x1, Pallas kernels, fused(): pl.pallas_call(functools.partial(pack_kernel, groups), out_shape=jax.Shap...  1.82 us

profile of v1, /device:TPU:0, one launch (start us, length us, event | category | flops | bytes accessed | tf_op | source)
XLA Modules:
  0.0 22.4 jit_solution(14321347193485735562)
XLA Ops:
  0.6 1.8 %pack.1 = bf16[256,512]{1,0:T(8,128)(2,1)} custom-call(s32[1,8]{1,0:T(1,128)} %bitcast.14, s32[1,8]{1,0:T(1,128)} %bitcast.15, bf16[16,1024]{1,0:T(8,128)(2,1)} %bitcast.12, f32[1,1024]{1,0:T(1,128)} %bitcast.13, f32[1,16]{1,0:T(1,128)} %bitcast.16), custom_call_target="tpu_custom_call" | custom-call | tf_op jit(solution)/shard_map/pack/pallas_call | solution.py:126
  2.5 18.0 %all_to_all.11 = bf16[32,8,512]{2,1,0:T(8,128)(2,1)} all-to-all(bf16[32,8,512]{2,1,0:T(8,128)(2,1)} %bitcast.11), channel_id=1, replica_groups=mesh['actors'=8,'rep'=4] {'actors','rep'}, dimensions={0} | all-to-all | bytes 524288 | tf_op jit(solution)/shard_map/all_to_all | solution.py:140
  20.5 1.9 %unpack.1 = (bf16[24,1024]{1,0:T(8,128)(2,1)}, f32[1,24]{1,0:T(1,128)}, s32[1,1]{1,0:T(1,128)}) custom-call(bf16[256,512]{1,0:T(8,128)(2,1)} %bitcast.10), custom_call_target="tpu_custom_call" | custom-call | tf_op jit(solution)/shard_map/unpack/pallas_call | solution.py:141

commit v2 on v0

--- a/solution.py
+++ b/solution.py
@@ -1,13 +1,207 @@
+import functools
+
 import jax
 import jax.numpy as jnp
 from jax import lax
+from jax.experimental import pallas as pl
+from jax.experimental.pallas import tpu as pltpu
 from jax.sharding import PartitionSpec as P
 
 CAP = 3
-
-
 EPS_NORM = 1e-06
 EPS_VAR = 1e-05
+
+LANES = 128
+SUBLANES = 8
+VMEM_GRANT = 8 << 20
+HIGH, MIDDLE, LOW, KEPT = range(4)
+
+
+def pack_kernel(
+    groups, length_hbm, owner_hbm, rows_hbm, gain_hbm, reward_hbm, out_ref,
+    length_ref, owner_ref, rows_ref, gain_ref, reward_ref, reward_at, start_of, length_of, sems,
+):
+    games = length_ref.shape[1]
+    row_count, width = rows_ref.shape
+    columns = out_ref.shape[2] // LANES - 1
+    across = width // LANES
+    copies = [
+        pltpu.make_async_copy(source, target, sems.at[n])
+        for n, (source, target) in enumerate(
+            (
+                (length_hbm, length_ref),
+                (owner_hbm, owner_ref),
+                (rows_hbm, rows_ref),
+                (gain_hbm, gain_ref),
+                (reward_hbm, reward_ref),
+                (reward_hbm, reward_at),
+            )
+        )
+    ]
+    for copy in copies:
+        copy.start()
+    mine, actor = lax.axis_index("rep"), lax.axis_index("actors")
+    actors = lax.axis_size("actors")
+    lane = lax.broadcasted_iota(jnp.int32, (SUBLANES, LANES), 1)
+    sublane = lax.broadcasted_iota(jnp.int32, (SUBLANES, LANES), 0)
+    for copy in copies:
+        copy.wait()
+
+    start = jnp.int32(0)
+    for game in range(games):
+        owner = owner_ref[0, game]
+        start_of[owner] = start
+        length_of[owner] = length_ref[0, game]
+        start = start + length_ref[0, game]
+
+    wide = rows_ref[...].astype(jnp.float32)
+    square_mean = jnp.sum(wide * wide, axis=1, keepdims=True) / width
+    normed = (wide * lax.rsqrt(square_mean + EPS_NORM) * gain_ref[...]).astype(jnp.bfloat16)
+    source = jnp.concatenate([normed[:, k * LANES : (k + 1) * LANES] for k in range(across)], axis=0)
+    lanes_of = lax.broadcasted_iota(jnp.int32, (SUBLANES, across * row_count), 1)
+    rows_of = lax.broadcasted_iota(jnp.int32, (SUBLANES, across * row_count), 0)
+    picks = []
+    for c in range(columns):
+        piece = rows_of * columns + c
+        position = piece // across
+        base = lanes_of - (piece % across) * row_count - position
+        for t in range(games):
+            hit = (base == start_of[t]) & (position < length_of[t])
+            picks.append(jnp.where(hit, 1.0, 0.0))
+    picked = jnp.dot(
+        jnp.concatenate(picks, axis=0).astype(jnp.bfloat16), source, preferred_element_type=jnp.float32
+    ).astype(jnp.bfloat16)
+    for c in range(columns):
+        for t in range(games):
+            at = (c * games + t) * SUBLANES
+            out_ref[t * groups + mine, :, c * LANES : (c + 1) * LANES] = picked[at : at + SUBLANES]
+
+    reward = reward_ref[...]
+    first = jnp.sum(reward, axis=1, keepdims=True)
+    second = jnp.sum(reward * reward, axis=1, keepdims=True)
+    common = jnp.where(lane == CAP * actors, first, jnp.where(lane == CAP * actors + 1, second, 0.0))
+    for t in range(games):
+        begin, size = start_of[t], length_of[t]
+        values = jnp.where(lane == CAP * actors + 2, size.astype(jnp.float32), common)
+        for j in range(CAP):
+            value = jnp.where(j < size, reward_at[0, jnp.minimum(begin + j, row_count - 1)], 0.0)
+            values = jnp.where(lane == CAP * actor + j, value, values)
+        high = values.astype(jnp.bfloat16).astype(jnp.float32)
+        middle = (values - high).astype(jnp.bfloat16).astype(jnp.float32)
+        low = values - high - middle
+        kept = jnp.where((lane >= CAP * actor) & (lane < CAP * actor + size), 1.0, 0.0)
+        tile = jnp.where(sublane == HIGH, high, 0.0)
+        tile = jnp.where(sublane == MIDDLE, middle, tile)
+        tile = jnp.where(sublane == LOW, low, tile)
+        tile = jnp.where(sublane == KEPT, kept, tile).astype(jnp.bfloat16)
+        for group in range(groups):
+            out_ref[t * groups + group, :, columns * LANES :] = tile
+
+
+def unpack_kernel(groups, rows_total, in_ref, rows_hbm, reward_hbm, count_hbm, rows_ref, reward_ref, count_ref, sems):
+    actors = in_ref.shape[0] // groups
+    columns = in_ref.shape[2] // LANES - 1
+    slots, width = rows_ref.shape
+    across = width // LANES
+    mine = lax.axis_index("rep")
+
+    depth = columns * actors * SUBLANES
+    pieces = jnp.concatenate(
+        [in_ref[s * groups + mine, :, c * LANES : (c + 1) * LANES] for c in range(columns) for s in range(actors)],
+        axis=0,
+    )
+    slot = lax.broadcasted_iota(jnp.int32, (slots, depth), 0)
+    column = lax.broadcasted_iota(jnp.int32, (slots, depth), 1)
+    actor, q = (column // SUBLANES) % actors, column % SUBLANES
+    piece = q * columns + column // (SUBLANES * actors)
+    piece = jnp.where(slot // CAP == actor, piece - (slot % CAP) * across, -1)
+    pick = jnp.concatenate([jnp.where(piece == k, 1.0, 0.0) for k in range(across)], axis=0)
+    got = jnp.dot(pick.astype(jnp.bfloat16), pieces, preferred_element_type=jnp.float32).astype(jnp.bfloat16)
+    for k in range(across):
+        rows_ref[:, k * LANES : (k + 1) * LANES] = got[k * slots : (k + 1) * slots]
+    rows_copy = pltpu.make_async_copy(rows_ref, rows_hbm, sems.at[0])
+    rows_copy.start()
+
+    def tile(block):
+        return in_ref[block, :, columns * LANES :].astype(jnp.float32)
+
+    own = sum(tile(s * groups + mine) for s in range(actors))
+    every = sum(tile(block) for block in range(actors * groups))
+    own_value = own[HIGH : HIGH + 1] + own[MIDDLE : MIDDLE + 1] + own[LOW : LOW + 1]
+    every_value = every[HIGH : HIGH + 1] + every[MIDDLE : MIDDLE + 1] + every[LOW : LOW + 1]
+    mean = every_value[:, slots : slots + 1] / rows_total
+    second = every_value[:, slots + 1 : slots + 2] / rows_total
+    scale = lax.rsqrt(second - mean * mean + EPS_VAR)
+    scaled = jnp.where(own[KEPT : KEPT + 1] > 0.5, (own_value - mean) * scale, 0.0)
+    reward_ref[...] = scaled[:, :slots]
+    count_ref[...] = every_value[:, slots + 2 : slots + 3].astype(jnp.int32)
+    reward_copy = pltpu.make_async_copy(reward_ref, reward_hbm, sems.at[1])
+    count_copy = pltpu.make_async_copy(count_ref, count_hbm, sems.at[2])
+    reward_copy.start()
+    count_copy.start()
+    rows_copy.wait()
+    reward_copy.wait()
+    count_copy.wait()
+
+
+def fused(features, rewards, lengths, owners, norm_gain):
+    row_count, width = features.shape[2:]
+    games = lengths.shape[2]
+    actors, groups = lax.axis_size("actors"), lax.axis_size("rep")
+    slots = actors * CAP
+    columns = CAP * width // (SUBLANES * LANES)
+    vmem = pl.BlockSpec(memory_space=pltpu.VMEM)
+    hbm = pl.BlockSpec(memory_space=pltpu.HBM)
+    packed = pl.pallas_call(
+        functools.partial(pack_kernel, groups),
+        out_shape=jax.ShapeDtypeStruct((games * groups, SUBLANES, (columns + 1) * LANES), jnp.bfloat16),
+        in_specs=[hbm] * 5,
+        out_specs=vmem,
+        scratch_shapes=[
+            pltpu.SMEM((1, games), jnp.int32),
+            pltpu.SMEM((1, games), jnp.int32),
+            pltpu.VMEM((row_count, width), jnp.bfloat16),
+            pltpu.VMEM((1, width), jnp.float32),
+            pltpu.VMEM((1, row_count), jnp.float32),
+            pltpu.SMEM((1, row_count), jnp.float32),
+            pltpu.SMEM((games,), jnp.int32),
+            pltpu.SMEM((games,), jnp.int32),
+            pltpu.SemaphoreType.DMA((6,)),
+        ],
+        compiler_params=pltpu.CompilerParams(vmem_limit_bytes=VMEM_GRANT),
+        name="pack",
+    )(
+        *(
+            pltpu.with_memory_space_constraint(x, pltpu.HBM)
+            for x in (
+                lengths.reshape(1, games),
+                owners.reshape(1, games),
+                features.reshape(row_count, width),
+                norm_gain.reshape(1, width),
+                rewards.reshape(1, row_count),
+            )
+        )
+    )
+    landed = lax.all_to_all(packed, ("actors", "rep"), split_axis=0, concat_axis=0, tiled=True)
+    rows, scaled, count = pl.pallas_call(
+        functools.partial(unpack_kernel, groups, row_count * actors * groups),
+        out_shape=(
+            jax.ShapeDtypeStruct((slots, width), jnp.bfloat16),
+            jax.ShapeDtypeStruct((1, slots), jnp.float32),
+            jax.ShapeDtypeStruct((1, 1), jnp.int32),
+        ),
+        in_specs=[vmem],
+        out_specs=(hbm, hbm, hbm),
+        scratch_shapes=[
+            pltpu.VMEM((slots, width), jnp.bfloat16),
+            pltpu.VMEM((1, slots), jnp.float32),
+            pltpu.VMEM((1, 1), jnp.int32),
+            pltpu.SemaphoreType.DMA((3,)),
+        ],
+        compiler_params=pltpu.CompilerParams(vmem_limit_bytes=VMEM_GRANT),
+        name="unpack",
+    )(landed)
+    return (rows.reshape(1, 1, -1, width), scaled.reshape(1, 1, -1), count.reshape(1))
 
 
 def rms_scale(rows, norm_gain):
@@ -16,7 +210,7 @@
     return (widened * lax.rsqrt(square_mean + EPS_NORM) * norm_gain).astype(jnp.bfloat16)
 
 
-def local(features, rewards, lengths, owners, norm_gain):
+def plain(features, rewards, lengths, owners, norm_gain):
     rows_here = features[0, 0]
     reward_here = rewards[0, 0]
     game_len = lengths[0, 0]
@@ -33,19 +227,12 @@
     slot_pos = jnp.arange(CAP, dtype=jnp.int32)
     usable = slot_pos[None, :] < held_len[:, None]
     row_index = jnp.minimum(held_start[:, None] + slot_pos[None, :], row_count - 1)
-    outgoing = jnp.where(
-        usable, jnp.take(reward_here, row_index, axis=0), jnp.zeros((), jnp.float32)
-    )
-    arrived, arrived_len = (
-        lax.all_to_all(outgoing, "actors", split_axis=0, concat_axis=0, tiled=True),
-        lax.all_to_all(
-            held_len.astype(jnp.float32)[:, None], "actors", split_axis=0, concat_axis=0, tiled=True
-        ),
-    )
+    outgoing = jnp.where(usable, jnp.take(reward_here, row_index, axis=0), jnp.zeros((), jnp.float32))
+    outgoing = jnp.concatenate([outgoing, held_len.astype(jnp.float32)[:, None]], axis=1)
+    arrived = lax.all_to_all(outgoing, "actors", split_axis=0, concat_axis=0, tiled=True)
+    arrived, arrived_len = arrived[:, :CAP], arrived[:, CAP:]
     normed = rms_scale(rows_here, norm_gain)
-    packed = jnp.where(
-        usable[:, :, None], jnp.take(normed, row_index, axis=0), jnp.zeros((), jnp.bfloat16)
-    )
+    packed = jnp.where(usable[:, :, None], jnp.take(normed, row_index, axis=0), jnp.zeros((), jnp.bfloat16))
     landed = lax.all_to_all(packed, "actors", split_axis=0, concat_axis=0, tiled=True)
     first, second = lax.psum((jnp.sum(arrived), jnp.sum(arrived * arrived)), ("actors", "rep"))
     reward_mean = first / row_total
@@ -55,6 +242,21 @@
     count_here = jnp.sum(arrived_len).astype(jnp.int32)
     counts = lax.psum(count_here, "rep")
     return (landed.reshape(1, 1, -1, width), scaled.reshape(1, 1, -1), counts.reshape(1))
+
+
+def local(features, rewards, lengths, owners, norm_gain):
+    actors, groups = lax.axis_size("actors"), lax.axis_size("rep")
+    row_count, width = features.shape[2:]
+    fits = (
+        actors * CAP + 3 <= LANES
+        and lengths.shape[2] == actors
+        and CAP * width % (SUBLANES * LANES) == 0
+        and row_count % 16 == 0
+        and row_count <= LANES
+        and actors % SUBLANES == 0
+    )
+    step = fused if fits else plain
+    return step(features, rewards, lengths, owners, norm_gain)
 
 
 def solution(mesh):

time: 79 us -> 20.5 us (0.26)
  blocking collectives: 46.4 us -> 17.7 us
  starting transfers between devices: 16.5 us -> 0 us
  other arithmetic: 4.59 us -> 0 us
  local copies, waits for them, and re-layouts: 3.69 us -> 0 us
  between operations: 4 us -> 0.64 us
  waiting for transfers between devices: 3.1 us -> 0 us
  Pallas kernels: 0 us -> 1.94 us
    psum x2 -> x0, blocking collectives: 46.4 us -> none  [the longest x1 40.3 us: local(): lax.psum((jnp.sum(arrived), jnp.sum(arrived * arrived)), ('actors', 'rep'))]
    all_to_all x0 -> x1, blocking collectives: none -> 17.7 us  [fused(): lax.all_to_all(packed, ('actors', 'rep'), split_axis=0, concat_axis=0, ti...]
    all_to_all x3 -> x0, starting transfers between devices: 16.5 us -> none  [the longest x1 7.31 us: local(): lax.all_to_all(held_len.astype(jnp.float32)[:, None], 'actors', split_axi...]
    all_to_all x3 -> x0, waiting for transfers between devices: 3.1 us -> none  [the longest x1 3.09 us: local(): lax.all_to_all(held_len.astype(jnp.float32)[:, None], 'actors', split_axi...]
    reduce_sum x4 -> x0, other arithmetic: 2.14 us -> none  [the longest x1 0.8 us: local(): held_len = jnp.sum(owns_game * game_len[None, :], axis=1)]
    select_n x4 -> x0, other arithmetic: 1.99 us -> none  [the longest x1 0.73 us: local(): jnp.where(usable[:, :, None], jnp.take(normed, row_index, axis=0), jnp.ze...]
    pallas_call x0 -> x2, Pallas kernels: none -> 1.94 us  [the longest x1 1.11 us: fused(): pl.pallas_call(functools.partial(pack_kernel, groups), out_shape=jax.Shap...]
    gather x4 -> x0, local copies, waits for them, and re-layouts: 1.42 us -> none  [the longest x2 0.78 us: local(): jnp.take(reward_here, row_index, axis=0)]
  transfers between devices with their start and end apart: 3 -> 0, of which waited for: 1 -> 0; matrix products, arithmetic and copies ran while one was open for 7% -> 0% of each run, Pallas kernels for 0% -> 0%
where the time goes in v2:
time: 20.5 us; the launch traced here: 20.3 us
  blocking collectives  17.7 us (86%)
  Pallas kernels  1.94 us (9%)
  between operations  0.64 us (3%)
    all_to_all x1, blocking collectives, fused(): lax.all_to_all(packed, ('actors', 'rep'), split_axis=0, concat_axis=0, ti...  17.7 us
    pallas_call x1, Pallas kernels, fused(): pl.pallas_call(functools.partial(pack_kernel, groups), out_shape=jax.Shap...  1.11 us
    pallas_call x1, Pallas kernels, fused(): pl.pallas_call(functools.partial(unpack_kernel, groups, row_count * actor...  0.83 us

profile of v2, /device:TPU:0, one launch (start us, length us, event | category | flops | bytes accessed | tf_op | source)
XLA Modules:
  0.0 20.3 jit_solution(14174459886625082055)
XLA Ops:
  0.6 1.1 %pack.1 = bf16[32,8,512]{2,1,0:T(8,128)(2,1)S(1)} custom-call(s32[1,8]{1,0:T(1,128)} %bitcast.10, s32[1,8]{1,0:T(1,128)} %bitcast.11, bf16[16,1024]{1,0:T(8,128)(2,1)} %bitcast.8, f32[1,1024]{1,0:T(1,128)} %bitcast.9, f32[1,16]{1,0:T(1,128)} %bitcast.12), custom_call_target="tpu_custom_call" | custom-call | tf_op jit(solution)/shard_map/pack/pallas_call | solution.py:155
  1.7 17.7 %all_to_all.5.in_ref = bf16[32,8,512]{2,1,0:T(8,128)(2,1)S(1)} all-to-all(bf16[32,8,512]{2,1,0:T(8,128)(2,1)S(1)} %pack.1), channel_id=1, replica_groups=mesh['actors'=8,'rep'=4] {'actors','rep'}, dimensions={0} | all-to-all | bytes 524288 | tf_op jit(solution)/shard_map/all_to_all | solution.py:185
  19.5 0.8 %unpack.1 = (bf16[24,1024]{1,0:T(8,128)(2,1)}, f32[1,24]{1,0:T(1,128)}, s32[1,1]{1,0:T(1,128)}) custom-call(bf16[32,8,512]{2,1,0:T(8,128)(2,1)S(1)} %all_to_all.5.in_ref), custom_call_target="tpu_custom_call" | custom-call | tf_op jit(solution)/shard_map/unpack/pallas_call | solution.py:186

commit v3 on v2

v3 whole, which is shorter than its diff:
```python
import functools

import jax
import jax.numpy as jnp
from jax import lax
from jax.experimental import pallas as pl
from jax.experimental.pallas import tpu as pltpu
from jax.sharding import PartitionSpec as P

CAP = 3
EPS_NORM = 1e-06
EPS_VAR = 1e-05

LANES = 128
SUBLANES = 8
PAIR = 2
HALF = LANES // 2
VMEM_GRANT = 8 << 20


def pack_kernel(
    groups, length_hbm, owner_hbm, rows_hbm, gain_hbm, reward_hbm, out_ref,
    length_ref, owner_ref, rows_ref, gain_ref, reward_ref, reward_at, normed_ref, scalar_ref, sems,
):
    games = length_ref.shape[1]
    row_count, width = rows_ref.shape
    across = width // LANES
    last = out_ref.shape[1] - 1
    copies = [
        pltpu.make_async_copy(source, target, sems.at[n])
        for n, (source, target) in enumerate(
            (
                (rows_hbm, rows_ref),
                (length_hbm, length_ref),
                (owner_hbm, owner_ref),
                (reward_hbm, reward_at),
                (reward_hbm, reward_ref),
                (gain_hbm, gain_ref),
            )
        )
    ]
    for copy in copies:
        copy.start()
    mine, actor = lax.axis_index("rep"), lax.axis_index("actors")
    slots = lax.axis_size("actors") * CAP
    lane = lax.broadcasted_iota(jnp.int32, (games, LANES), 1)
    place = lane % HALF
    trainer = lax.broadcasted_iota(jnp.int32, (games, LANES), 0)
    for copy in copies:
        copy.wait()

    wide = rows_ref[...].astype(jnp.float32)
    square_mean = jnp.sum(wide * wide, axis=1, keepdims=True) / width
    normed = wide * lax.rsqrt(square_mean + EPS_NORM) * gain_ref[...]
    for k in range(across):
        normed_ref[k * row_count : (k + 1) * row_count] = normed[:, k * LANES : (k + 1) * LANES]

    reward = reward_ref[...]
    first = jnp.sum(reward, axis=1, keepdims=True)
    second = jnp.sum(reward * reward, axis=1, keepdims=True)
    values = jnp.where(place == slots, first, jnp.where(place == slots + 1, second, 0.0))
    sizes = jnp.zeros((games, LANES), jnp.int32)
    start = jnp.int32(0)
    for game in range(games):
        owner, size = owner_ref[0, game], length_ref[0, game]
        chosen = trainer == owner
        sizes = jnp.where(chosen, size, sizes)
        parts = []
        for j in range(CAP):
            part = normed_ref[pl.ds(start + j, across, stride=row_count), :]
            parts.append(jnp.where(j < size, part, 0.0))
            value = reward_at[0, jnp.minimum(start + j, row_count - 1)]
            values = jnp.where(chosen & (place == CAP * actor + j) & (j < size), value, values)
        block = jnp.concatenate(parts, axis=0).astype(jnp.bfloat16)
        out_ref[owner * groups + mine, :last] = block.reshape(last, PAIR, LANES)
        start = start + size

    values = jnp.where(place == slots + 2, sizes.astype(jnp.float32), values)
    high = values.astype(jnp.bfloat16).astype(jnp.float32)
    middle = (values - high).astype(jnp.bfloat16).astype(jnp.float32)
    low = values - high - middle
    kept = jnp.where((place >= CAP * actor) & (place < CAP * actor + sizes), 1.0, 0.0)
    scalar_ref[pl.ds(0, games, stride=PAIR), :] = jnp.where(lane < HALF, high, middle)
    scalar_ref[pl.ds(1, games, stride=PAIR), :] = jnp.where(lane < HALF, low, kept)
    tiles = scalar_ref[...].astype(jnp.bfloat16).reshape(games, PAIR, LANES)
    for t in range(games):
        for group in range(groups):
            out_ref[t * groups + group, last] = tiles[t]


def unpack_kernel(
    groups, rows_total, in_ref, rows_hbm, reward_hbm, count_hbm, rows_ref, reward_ref, count_ref, piece_ref, sems
):
    actors = in_ref.shape[0] // groups
    last = in_ref.shape[1] - 1
    slots, width = rows_ref.shape
    across = width // LANES
    mine = lax.axis_index("rep")

    for s in range(actors):
        block = in_ref[s * groups + mine, :last].reshape(last * PAIR, LANES)
        piece_ref[s * last * PAIR : (s + 1) * last * PAIR] = block.astype(jnp.float32)
    for k in range(across):
        lanes = piece_ref[pl.ds(k, slots, stride=across), :]
        rows_ref[:, k * LANES : (k + 1) * LANES] = lanes.astype(jnp.bfloat16)
    rows_copy = pltpu.make_async_copy(rows_ref, rows_hbm, sems.at[0])
    rows_copy.start()

    def tile(block):
        return in_ref[block, last].astype(jnp.float32)

    def value(total):
        return total[:1, :HALF] + total[:1, HALF:] + total[1:, :HALF]

    own = sum(tile(s * groups + mine) for s in range(actors))
    every = value(sum(tile(block) for block in range(actors * groups)))
    mean = every[:, slots : slots + 1] / rows_total
    second = every[:, slots + 1 : slots + 2] / rows_total
    scale = lax.rsqrt(second - mean * mean + EPS_VAR)
    scaled = jnp.where(own[1:, HALF:] > 0.5, (value(own) - mean) * scale, 0.0)
    reward_ref[...] = scaled[:, :slots]
    count_ref[...] = every[:, slots + 2 : slots + 3].astype(jnp.int32)
    reward_copy = pltpu.make_async_copy(reward_ref, reward_hbm, sems.at[1])
    count_copy = pltpu.make_async_copy(count_ref, count_hbm, sems.at[2])
    reward_copy.start()
    count_copy.start()
    rows_copy.wait()
    reward_copy.wait()
    count_copy.wait()


def fused(features, rewards, lengths, owners, norm_gain):
    row_count, width = features.shape[2:]
    games = lengths.shape[2]
    actors, groups = lax.axis_size("actors"), lax.axis_size("rep")
    slots = actors * CAP
    across = width // LANES
    last = CAP * across // PAIR
    vmem = pl.BlockSpec(memory_space=pltpu.VMEM)
    hbm = pl.BlockSpec(memory_space=pltpu.HBM)
    packed = pl.pallas_call(
        functools.partial(pack_kernel, groups),
        out_shape=jax.ShapeDtypeStruct((games * groups, last + 1, PAIR, LANES), jnp.bfloat16),
        in_specs=[hbm] * 5,
        out_specs=vmem,
        scratch_shapes=[
            pltpu.SMEM((1, games), jnp.int32),
            pltpu.SMEM((1, games), jnp.int32),
            pltpu.VMEM((row_count, width), jnp.bfloat16),
            pltpu.VMEM((1, width), jnp.float32),
            pltpu.VMEM((1, row_count), jnp.float32),
            pltpu.SMEM((1, row_count), jnp.float32),
            pltpu.VMEM(((across + 1) * row_count, LANES), jnp.float32),
            pltpu.VMEM((PAIR * games, LANES), jnp.float32),
            pltpu.SemaphoreType.DMA((6,)),
        ],
        compiler_params=pltpu.CompilerParams(vmem_limit_bytes=VMEM_GRANT),
        name="pack",
    )(
        *(
            pltpu.with_memory_space_constraint(x, pltpu.HBM)
            for x in (
                lengths.reshape(1, games),
                owners.reshape(1, games),
                features.reshape(row_count, width),
                norm_gain.reshape(1, width),
                rewards.reshape(1, row_count),
            )
        )
    )
    landed = lax.all_to_all(packed, ("actors", "rep"), split_axis=0, concat_axis=0, tiled=True)
    rows, scaled, count = pl.pallas_call(
        functools.partial(unpack_kernel, groups, row_count * actors * groups),
        out_shape=(
            jax.ShapeDtypeStruct((slots, width), jnp.bfloat16),
            jax.ShapeDtypeStruct((1, slots), jnp.float32),
            jax.ShapeDtypeStruct((1, 1), jnp.int32),
        ),
        in_specs=[vmem],
        out_specs=(hbm, hbm, hbm),
        scratch_shapes=[
            pltpu.VMEM((slots, width), jnp.bfloat16),
            pltpu.VMEM((1, slots), jnp.float32),
            pltpu.VMEM((1, 1), jnp.int32),
            pltpu.VMEM((slots * across, LANES), jnp.float32),
            pltpu.SemaphoreType.DMA((3,)),
        ],
        compiler_params=pltpu.CompilerParams(vmem_limit_bytes=VMEM_GRANT),
        name="unpack",
    )(landed)
    return (rows.reshape(1, 1, -1, width), scaled.reshape(1, 1, -1), count.reshape(1))


def rms_scale(rows, norm_gain):
    widened = rows.astype(jnp.float32)
    square_mean = jnp.mean(widened * widened, axis=-1, keepdims=True)
    return (widened * lax.rsqrt(square_mean + EPS_NORM) * norm_gain).astype(jnp.bfloat16)


def plain(features, rewards, lengths, owners, norm_gain):
    rows_here = features[0, 0]
    reward_here = rewards[0, 0]
    game_len = lengths[0, 0]
    game_owner = owners[0, 0]
    games = game_len.shape[0]
    row_count = rows_here.shape[0]
    width = rows_here.shape[1]
    row_total = row_count * lax.axis_size("actors") * lax.axis_size("rep")
    starts = jnp.cumsum(game_len) - game_len
    trainer_ids = jnp.arange(games, dtype=jnp.int32)
    owns_game = (game_owner[None, :] == trainer_ids[:, None]).astype(jnp.int32)
    held_len = jnp.sum(owns_game * game_len[None, :], axis=1)
    held_start = jnp.sum(owns_game * starts[None, :], axis=1)
    slot_pos = jnp.arange(CAP, dtype=jnp.int32)
    usable = slot_pos[None, :] < held_len[:, None]
    row_index = jnp.minimum(held_start[:, None] + slot_pos[None, :], row_count - 1)
    outgoing = jnp.where(usable, jnp.take(reward_here, row_index, axis=0), jnp.zeros((), jnp.float32))
    outgoing = jnp.concatenate([outgoing, held_len.astype(jnp.float32)[:, None]], axis=1)
    arrived = lax.all_to_all(outgoing, "actors", split_axis=0, concat_axis=0, tiled=True)
    arrived, arrived_len = arrived[:, :CAP], arrived[:, CAP:]
    normed = rms_scale(rows_here, norm_gain)
    packed = jnp.where(usable[:, :, None], jnp.take(normed, row_index, axis=0), jnp.zeros((), jnp.bfloat16))
    landed = lax.all_to_all(packed, "actors", split_axis=0, concat_axis=0, tiled=True)
    first, second = lax.psum((jnp.sum(arrived), jnp.sum(arrived * arrived)), ("actors", "rep"))
    reward_mean = first / row_total
    inv_spread = lax.rsqrt(second / row_total - reward_mean * reward_mean + EPS_VAR)
    keep_slot = slot_pos[None, :].astype(jnp.float32) < arrived_len
    scaled = jnp.where(keep_slot, (arrived - reward_mean) * inv_spread, jnp.zeros((), jnp.float32))
    count_here = jnp.sum(arrived_len).astype(jnp.int32)
    counts = lax.psum(count_here, "rep")
    return (landed.reshape(1, 1, -1, width), scaled.reshape(1, 1, -1), counts.reshape(1))


def local(features, rewards, lengths, owners, norm_gain):
    actors, groups = lax.axis_size("actors"), lax.axis_size("rep")
    row_count, width = features.shape[2:]
    fits = (
        actors * CAP + 3 <= HALF
        and lengths.shape[2] == actors
        and actors % SUBLANES == 0
        and width % (SUBLANES * LANES) == 0
        and row_count % 16 == 0
        and row_count <= LANES
    )
    step = fused if fits else plain
    return step(features, rewards, lengths, owners, norm_gain)


def solution(mesh):
    return jax.shard_map(
        local,
        mesh=mesh,
        in_specs=(
            P("rep", "actors", None, None),
            P("rep", "actors", None),
            P("rep", "actors", None),
            P("rep", "actors", None),
            P(),
        ),
        out_specs=(P("rep", "actors", None, None), P("rep", "actors", None), P("actors")),
        check_vma=False,
    )
```

time: 20.5 us -> 19.4 us (0.946)
  blocking collectives: 17.7 us -> 16.6 us
    all_to_all x1, blocking collectives: 17.7 us -> 16.6 us  [fused(): lax.all_to_all(packed, ('actors', 'rep'), split_axis=0, concat_axis=0, ti...]
where the time goes in v3:
time: 19.4 us; the launch traced here: 19.2 us
  blocking collectives  16.6 us (86%)
  Pallas kernels  2.04 us (11%)
  between operations  0.64 us (3%)
    all_to_all x1, blocking collectives, fused(): lax.all_to_all(packed, ('actors', 'rep'), split_axis=0, concat_axis=0, ti...  16.6 us
    pallas_call x1, Pallas kernels, fused(): pl.pallas_call(functools.partial(pack_kernel, groups), out_shape=jax.Shap...  1.05 us
    pallas_call x1, Pallas kernels, fused(): pl.pallas_call(functools.partial(unpack_kernel, groups, row_count * actor...  0.99 us

profile of v3, /device:TPU:0, one launch (start us, length us, event | category | flops | bytes accessed | tf_op | source)
XLA Modules:
  0.0 19.2 jit_solution(15833257827340198879)
XLA Ops:
  0.6 1.1 %pack.1 = bf16[32,13,2,128]{3,2,1,0:T(2,128)(2,1)S(1)} custom-call(s32[1,8]{1,0:T(1,128)} %bitcast.10, s32[1,8]{1,0:T(1,128)} %bitcast.11, bf16[16,1024]{1,0:T(8,128)(2,1)} %bitcast.8, f32[1,1024]{1,0:T(1,128)} %bitcast.9, f32[1,16]{1,0:T(1,128)} %bitcast.12), custom_call_target="tpu_custom_call" | custom-call | tf_op jit(solution)/shard_map/pack/pallas_call | solution.py:141
  1.7 16.6 %all_to_all.5.in_ref = bf16[32,13,2,128]{3,2,1,0:T(2,128)(2,1)S(1)} all-to-all(bf16[32,13,2,128]{3,2,1,0:T(2,128)(2,1)S(1)} %pack.1), channel_id=1, replica_groups=mesh['actors'=8,'rep'=4] {'actors','rep'}, dimensions={0} | all-to-all | bytes 425984 | tf_op jit(solution)/shard_map/all_to_all | solution.py:171
  18.2 1.0 %unpack.1 = (bf16[24,1024]{1,0:T(8,128)(2,1)}, f32[1,24]{1,0:T(1,128)}, s32[1,1]{1,0:T(1,128)}) custom-call(bf16[32,13,2,128]{3,2,1,0:T(2,128)(2,1)S(1)} %all_to_all.5.in_ref), custom_call_target="tpu_custom_call" | custom-call | tf_op jit(solution)/shard_map/unpack/pallas_call | solution.py:172

commit v4 on v3

--- a/solution.py
+++ b/solution.py
@@ -16,103 +16,113 @@
 PAIR = 2
 HALF = LANES // 2
 VMEM_GRANT = 8 << 20
+ORDERS = {}
+
+
+def places(actors, groups):
+    order = ORDERS.get((actors, groups)) or [a * groups + g for g in range(groups) for a in range(actors)]
+    return order, [order.index(device) for device in range(actors * groups)]
+
+
+def of_group(choices, mine):
+    chosen = jnp.int32(choices[0])
+    for group in range(1, len(choices)):
+        chosen = jnp.where(mine == group, choices[group], chosen)
+    return chosen
 
 
 def pack_kernel(
-    groups, length_hbm, owner_hbm, rows_hbm, gain_hbm, reward_hbm, out_ref,
-    length_ref, owner_ref, rows_ref, gain_ref, reward_ref, reward_at, normed_ref, scalar_ref, sems,
+    place_of, groups, length_ref, owner_ref, reward_at, rows_ref, gain_ref, reward_ref,
+    out_ref, normed_ref, scalar_ref, start_of, length_of,
 ):
     games = length_ref.shape[1]
     row_count, width = rows_ref.shape
     across = width // LANES
+    stride = row_count
     last = out_ref.shape[1] - 1
-    copies = [
-        pltpu.make_async_copy(source, target, sems.at[n])
-        for n, (source, target) in enumerate(
-            (
-                (rows_hbm, rows_ref),
-                (length_hbm, length_ref),
-                (owner_hbm, owner_ref),
-                (reward_hbm, reward_at),
-                (reward_hbm, reward_ref),
-                (gain_hbm, gain_ref),
-            )
-        )
-    ]
-    for copy in copies:
-        copy.start()
     mine, actor = lax.axis_index("rep"), lax.axis_index("actors")
     slots = lax.axis_size("actors") * CAP
-    lane = lax.broadcasted_iota(jnp.int32, (games, LANES), 1)
-    place = lane % HALF
-    trainer = lax.broadcasted_iota(jnp.int32, (games, LANES), 0)
-    for copy in copies:
-        copy.wait()
+
+    start = jnp.int32(0)
+    for game in range(games):
+        owner, size = owner_ref[0, game], length_ref[0, game]
+        start_of[owner] = start
+        length_of[owner] = size
+        start = start + size
 
     wide = rows_ref[...].astype(jnp.float32)
     square_mean = jnp.sum(wide * wide, axis=1, keepdims=True) / width
     normed = wide * lax.rsqrt(square_mean + EPS_NORM) * gain_ref[...]
     for k in range(across):
-        normed_ref[k * row_count : (k + 1) * row_count] = normed[:, k * LANES : (k + 1) * LANES]
-
+        normed_ref[k * stride : k * stride + row_count] = normed[:, k * LANES : (k + 1) * LANES]
+
+    lane = lax.broadcasted_iota(jnp.int32, (games, LANES), 1)
+    place = lane % HALF
+    trainer = lax.broadcasted_iota(jnp.int32, (games, LANES), 0)
     reward = reward_ref[...]
     first = jnp.sum(reward, axis=1, keepdims=True)
     second = jnp.sum(reward * reward, axis=1, keepdims=True)
-    values = jnp.where(place == slots, first, jnp.where(place == slots + 1, second, 0.0))
     sizes = jnp.zeros((games, LANES), jnp.int32)
-    start = jnp.int32(0)
-    for game in range(games):
-        owner, size = owner_ref[0, game], length_ref[0, game]
-        chosen = trainer == owner
-        sizes = jnp.where(chosen, size, sizes)
+    held = [jnp.zeros((games, LANES), jnp.float32) for _ in range(CAP)]
+    for t in range(games):
+        begin, size = start_of[t], length_of[t]
+        sizes = jnp.where(trainer == t, size, sizes)
         parts = []
         for j in range(CAP):
-            part = normed_ref[pl.ds(start + j, across, stride=row_count), :]
+            part = normed_ref[pl.ds(begin + j, across, stride=stride), :]
             parts.append(jnp.where(j < size, part, 0.0))
-            value = reward_at[0, jnp.minimum(start + j, row_count - 1)]
-            values = jnp.where(chosen & (place == CAP * actor + j) & (j < size), value, values)
+            value = reward_at[0, jnp.minimum(begin + j, row_count - 1)]
+            held[j] = jnp.where(trainer == t, value, held[j])
         block = jnp.concatenate(parts, axis=0).astype(jnp.bfloat16)
-        out_ref[owner * groups + mine, :last] = block.reshape(last, PAIR, LANES)
-        start = start + size
-
+        target = of_group([place_of[t * groups + group] for group in range(groups)], mine)
+        out_ref[target, :last] = block.reshape(last, PAIR, LANES)
+
+    own = place - CAP * actor
+    kept = (own >= 0) & (own < sizes)
+    values = jnp.where(place == slots, first, jnp.where(place == slots + 1, second, 0.0))
     values = jnp.where(place == slots + 2, sizes.astype(jnp.float32), values)
+    for j in range(CAP):
+        values = jnp.where(kept & (own == j), held[j], values)
     high = values.astype(jnp.bfloat16).astype(jnp.float32)
     middle = (values - high).astype(jnp.bfloat16).astype(jnp.float32)
     low = values - high - middle
-    kept = jnp.where((place >= CAP * actor) & (place < CAP * actor + sizes), 1.0, 0.0)
     scalar_ref[pl.ds(0, games, stride=PAIR), :] = jnp.where(lane < HALF, high, middle)
-    scalar_ref[pl.ds(1, games, stride=PAIR), :] = jnp.where(lane < HALF, low, kept)
+    scalar_ref[pl.ds(1, games, stride=PAIR), :] = jnp.where(lane < HALF, low, jnp.where(kept, 1.0, 0.0))
     tiles = scalar_ref[...].astype(jnp.bfloat16).reshape(games, PAIR, LANES)
     for t in range(games):
         for group in range(groups):
-            out_ref[t * groups + group, last] = tiles[t]
+            out_ref[place_of[t * groups + group], last] = tiles[t]
 
 
 def unpack_kernel(
-    groups, rows_total, in_ref, rows_hbm, reward_hbm, count_hbm, rows_ref, reward_ref, count_ref, piece_ref, sems
+    place_of, groups, rows_total, in_ref, rows_hbm, reward_hbm, count_hbm, rows_ref, reward_ref, count_ref, piece_ref, sems
 ):
     actors = in_ref.shape[0] // groups
     last = in_ref.shape[1] - 1
     slots, width = rows_ref.shape
     across = width // LANES
+    stride = across
     mine = lax.axis_index("rep")
+    own_places = [of_group([place_of[s * groups + group] for group in range(groups)], mine) for s in range(actors)]
+
+    def tile(block):
+        return in_ref[block, last].astype(jnp.float32)
+
+    def value(total):
+        return total[:1, :HALF] + total[:1, HALF:] + total[1:, :HALF]
 
     for s in range(actors):
-        block = in_ref[s * groups + mine, :last].reshape(last * PAIR, LANES)
-        piece_ref[s * last * PAIR : (s + 1) * last * PAIR] = block.astype(jnp.float32)
+        block = in_ref[own_places[s], :last].reshape(last * PAIR, LANES).astype(jnp.float32)
+        for j in range(CAP):
+            at = (s * CAP + j) * stride
+            piece_ref[at : at + across] = block[j * across : (j + 1) * across]
     for k in range(across):
-        lanes = piece_ref[pl.ds(k, slots, stride=across), :]
+        lanes = piece_ref[pl.ds(k, slots, stride=stride), :]
         rows_ref[:, k * LANES : (k + 1) * LANES] = lanes.astype(jnp.bfloat16)
     rows_copy = pltpu.make_async_copy(rows_ref, rows_hbm, sems.at[0])
     rows_copy.start()
 
-    def tile(block):
-        return in_ref[block, last].astype(jnp.float32)
-
-    def value(total):
-        return total[:1, :HALF] + total[:1, HALF:] + total[1:, :HALF]
-
-    own = sum(tile(s * groups + mine) for s in range(actors))
+    own = sum(tile(block) for block in own_places)
     every = value(sum(tile(block) for block in range(actors * groups)))
     mean = every[:, slots : slots + 1] / rows_total
     second = every[:, slots + 1 : slots + 2] / rows_total
@@ -136,23 +146,20 @@
     slots = actors * CAP
     across = width // LANES
     last = CAP * across // PAIR
+    order, place_of = places(actors, groups)
     vmem = pl.BlockSpec(memory_space=pltpu.VMEM)
+    smem = pl.BlockSpec(memory_space=pltpu.SMEM)
     hbm = pl.BlockSpec(memory_space=pltpu.HBM)
     packed = pl.pallas_call(
-        functools.partial(pack_kernel, groups),
+        functools.partial(pack_kernel, place_of, groups),
         out_shape=jax.ShapeDtypeStruct((games * groups, last + 1, PAIR, LANES), jnp.bfloat16),
-        in_specs=[hbm] * 5,
+        in_specs=[smem, smem, smem, vmem, vmem, vmem],
         out_specs=vmem,
         scratch_shapes=[
-            pltpu.SMEM((1, games), jnp.int32),
-            pltpu.SMEM((1, games), jnp.int32),
-            pltpu.VMEM((row_count, width), jnp.bfloat16),
-            pltpu.VMEM((1, width), jnp.float32),
-            pltpu.VMEM((1, row_count), jnp.float32),
-            pltpu.SMEM((1, row_count), jnp.float32),
             pltpu.VMEM(((across + 1) * row_count, LANES), jnp.float32),
             pltpu.VMEM((PAIR * games, LANES), jnp.float32),
-            pltpu.SemaphoreType.DMA((6,)),
+            pltpu.SMEM((games,), jnp.int32),
+            pltpu.SMEM((games,), jnp.int32),
         ],
         compiler_params=pltpu.CompilerParams(vmem_limit_bytes=VMEM_GRANT),
         name="pack",
@@ -162,15 +169,18 @@
             for x in (
                 lengths.reshape(1, games),
                 owners.reshape(1, games),
+                rewards.reshape(1, row_count),
                 features.reshape(row_count, width),
                 norm_gain.reshape(1, width),
                 rewards.reshape(1, row_count),
             )
         )
     )
-    landed = lax.all_to_all(packed, ("actors", "rep"), split_axis=0, concat_axis=0, tiled=True)
+    landed = lax.all_to_all(
+        packed, ("actors", "rep"), split_axis=0, concat_axis=0, tiled=True, axis_index_groups=[order]
+    )
     rows, scaled, count = pl.pallas_call(
-        functools.partial(unpack_kernel, groups, row_count * actors * groups),
+        functools.partial(unpack_kernel, place_of, groups, row_count * actors * groups),
         out_shape=(
             jax.ShapeDtypeStruct((slots, width), jnp.bfloat16),
             jax.ShapeDtypeStruct((1, slots), jnp.float32),

time: 19.4 us -> 18.6 us (0.959)
  blocking collectives: 16.6 us -> 15.9 us
    all_to_all x1, blocking collectives: 16.6 us -> 15.9 us  [fused(): lax.all_to_all(packed, ('actors', 'rep'), split_axis=0, concat_axis=0, ti...]
where the time goes in v4:
time: 18.6 us; the launch traced here: 18.4 us
  blocking collectives  15.9 us (85%)
  Pallas kernels  1.92 us (10%)
  between operations  0.64 us (3%)
    all_to_all x1, blocking collectives, fused(): lax.all_to_all(packed, ('actors', 'rep'), split_axis=0, concat_axis=0, ti...  15.9 us
    pallas_call x1, Pallas kernels, fused(): pl.pallas_call(functools.partial(pack_kernel, place_of, groups), out_shap...  0.99 us
    pallas_call x1, Pallas kernels, fused(): pl.pallas_call(functools.partial(unpack_kernel, place_of, groups, row_cou...  0.93 us

profile of v4, /device:TPU:0, one launch (start us, length us, event | category | flops | bytes accessed | tf_op | source)
XLA Modules:
  0.0 18.4 jit_solution(12336266741672894742)
XLA Ops:
  0.6 1.0 %pack.1 = bf16[32,13,2,128]{3,2,1,0:T(2,128)(2,1)S(1)} custom-call(s32[1,8]{1,0:T(1,128)} %bitcast.12, s32[1,8]{1,0:T(1,128)} %bitcast.13, f32[1,16]{1,0:T(1,128)} %bitcast.10, bf16[16,1024]{1,0:T(8,128)(2,1)} %bitcast.8, f32[1,1024]{1,0:T(1,128)} %bitcast.9, f32[1,16]{1,0:T(1,128)} %bitcast.11), custom_call_target="tpu_custom_call" | custom-call | tf_op jit(solution)/shard_map/pack/pallas_call | solution.py:153
  1.6 15.9 %all_to_all.5.in_ref = bf16[32,13,2,128]{3,2,1,0:T(2,128)(2,1)S(1)} all-to-all(bf16[32,13,2,128]{3,2,1,0:T(2,128)(2,1)S(1)} %pack.1), channel_id=1, replica_groups={{0,4,8,12,16,20,24,28,1,5,9,13,17,21,25,29,2,6,10,14,18,22,26,30,3,7,11..., dimensions={0} | all-to-all | bytes 425984 | tf_op jit(solution)/shard_map/all_to_all | solution.py:179
  17.5 0.9 %unpack.1 = (bf16[24,1024]{1,0:T(8,128)(2,1)}, f32[1,24]{1,0:T(1,128)}, s32[1,1]{1,0:T(1,128)}) custom-call(bf16[32,13,2,128]{3,2,1,0:T(2,128)(2,1)S(1)} %all_to_all.5.in_ref), custom_call_target="tpu_custom_call" | custom-call | tf_op jit(solution)/shard_map/unpack/pallas_call | solution.py:182

commit v5 on v4

--- a/solution.py
+++ b/solution.py
@@ -16,7 +16,11 @@
 PAIR = 2
 HALF = LANES // 2
 VMEM_GRANT = 8 << 20
-ORDERS = {}
+ORDERS = {
+    (8, 4): [
+        4, 7, 18, 5, 27, 2, 16, 8, 21, 9, 30, 15, 17, 12, 29, 22, 3, 26, 6, 1, 11, 0, 13, 19, 24, 25, 31, 10, 23, 28, 14, 20,
+    ]
+}
 
 
 def places(actors, groups):

time: 18.6 us -> 17.5 us (0.941); the launches traced: 18.4 us -> 17.1 us
  blocking collectives: 15.9 us -> 14.6 us
    all_to_all x1, blocking collectives: 15.9 us -> 14.6 us  [fused(): lax.all_to_all(packed, ('actors', 'rep'), split_axis=0, concat_axis=0, ti...]
where the time goes in v5:
time: 17.5 us; the launch traced here: 17.1 us
  blocking collectives  14.6 us (83%)
  Pallas kernels  1.92 us (11%)
  between operations  0.64 us (4%)
    all_to_all x1, blocking collectives, fused(): lax.all_to_all(packed, ('actors', 'rep'), split_axis=0, concat_axis=0, ti...  14.6 us
    pallas_call x1, Pallas kernels, fused(): pl.pallas_call(functools.partial(pack_kernel, place_of, groups), out_shap...  0.99 us
    pallas_call x1, Pallas kernels, fused(): pl.pallas_call(functools.partial(unpack_kernel, place_of, groups, row_cou...  0.93 us

profile of v5, /device:TPU:0, one launch (start us, length us, event | category | flops | bytes accessed | tf_op | source)
XLA Modules:
  0.0 17.1 jit_solution(6061694617267921607)
XLA Ops:
  0.6 1.0 %pack.1 = bf16[32,13,2,128]{3,2,1,0:T(2,128)(2,1)S(1)} custom-call(s32[1,8]{1,0:T(1,128)} %bitcast.12, s32[1,8]{1,0:T(1,128)} %bitcast.13, f32[1,16]{1,0:T(1,128)} %bitcast.10, bf16[16,1024]{1,0:T(8,128)(2,1)} %bitcast.8, f32[1,1024]{1,0:T(1,128)} %bitcast.9, f32[1,16]{1,0:T(1,128)} %bitcast.11), custom_call_target="tpu_custom_call" | custom-call | tf_op jit(solution)/shard_map/pack/pallas_call | solution.py:157
  1.6 14.6 %all_to_all.5.in_ref = bf16[32,13,2,128]{3,2,1,0:T(2,128)(2,1)S(1)} all-to-all(bf16[32,13,2,128]{3,2,1,0:T(2,128)(2,1)S(1)} %pack.1), channel_id=1, replica_groups={{4,7,18,5,27,2,16,8,21,9,30,15,17,12,29,22,3,26,6,1,11,0,13,19,24,25,31..., dimensions={0} | all-to-all | bytes 425984 | tf_op jit(solution)/shard_map/all_to_all | solution.py:183
  16.2 0.9 %unpack.1 = (bf16[24,1024]{1,0:T(8,128)(2,1)}, f32[1,24]{1,0:T(1,128)}, s32[1,1]{1,0:T(1,128)}) custom-call(bf16[32,13,2,128]{3,2,1,0:T(2,128)(2,1)S(1)} %all_to_all.5.in_ref), custom_call_target="tpu_custom_call" | custom-call | tf_op jit(solution)/shard_map/unpack/pallas_call | solution.py:186

commit v6 on v5

--- a/solution.py
+++ b/solution.py
@@ -18,7 +18,7 @@
 VMEM_GRANT = 8 << 20
 ORDERS = {
     (8, 4): [
-        4, 7, 18, 5, 27, 2, 16, 8, 21, 9, 30, 15, 17, 12, 29, 22, 3, 26, 6, 1, 11, 0, 13, 19, 24, 25, 31, 10, 23, 28, 14, 20,
+        7, 18, 5, 14, 2, 16, 29, 21, 27, 30, 15, 17, 12, 6, 22, 3, 28, 10, 1, 11, 0, 13, 19, 24, 9, 31, 4, 23, 26, 25, 20, 8,
     ]
 }
 
@@ -99,7 +99,7 @@
 
 
 def unpack_kernel(
-    place_of, groups, rows_total, in_ref, rows_hbm, reward_hbm, count_hbm, rows_ref, reward_ref, count_ref, piece_ref, sems
+    place_of, groups, rows_total, in_ref, rows_ref, reward_ref, count_ref, piece_ref
 ):
     actors = in_ref.shape[0] // groups
     last = in_ref.shape[1] - 1
@@ -109,11 +109,11 @@
     mine = lax.axis_index("rep")
     own_places = [of_group([place_of[s * groups + group] for group in range(groups)], mine) for s in range(actors)]
 
-    def tile(block):
-        return in_ref[block, last].astype(jnp.float32)
-
-    def value(total):
-        return total[:1, :HALF] + total[:1, HALF:] + total[1:, :HALF]
+    def total(blocks):
+        terms = [in_ref[block, last].astype(jnp.float32) for block in blocks]
+        while len(terms) > 1:
+            terms = [sum(terms[at : at + 2]) for at in range(0, len(terms), 2)]
+        return terms[0]
 
     for s in range(actors):
         block = in_ref[own_places[s], :last].reshape(last * PAIR, LANES).astype(jnp.float32)
@@ -123,24 +123,22 @@
     for k in range(across):
         lanes = piece_ref[pl.ds(k, slots, stride=stride), :]
         rows_ref[:, k * LANES : (k + 1) * LANES] = lanes.astype(jnp.bfloat16)
-    rows_copy = pltpu.make_async_copy(rows_ref, rows_hbm, sems.at[0])
-    rows_copy.start()
-
-    own = sum(tile(block) for block in own_places)
-    every = value(sum(tile(block) for block in range(actors * groups)))
-    mean = every[:, slots : slots + 1] / rows_total
-    second = every[:, slots + 1 : slots + 2] / rows_total
+
+    every = total(range(actors * groups))
+    own = total(own_places)
+
+    def sum_of(at):
+        parts = (every[:1, at : at + 1], every[:1, HALF + at : HALF + at + 1], every[1:, at : at + 1])
+        high, middle, low = (jnp.broadcast_to(part, (1, HALF)) for part in parts)
+        return high + middle + low
+
+    mean = sum_of(slots) / rows_total
+    second = sum_of(slots + 1) / rows_total
     scale = lax.rsqrt(second - mean * mean + EPS_VAR)
-    scaled = jnp.where(own[1:, HALF:] > 0.5, (value(own) - mean) * scale, 0.0)
+    value = own[:1, :HALF] + own[:1, HALF:] + own[1:, :HALF]
+    scaled = jnp.where(own[1:, HALF:] > 0.5, (value - mean) * scale, 0.0)
     reward_ref[...] = scaled[:, :slots]
-    count_ref[...] = every[:, slots + 2 : slots + 3].astype(jnp.int32)
-    reward_copy = pltpu.make_async_copy(reward_ref, reward_hbm, sems.at[1])
-    count_copy = pltpu.make_async_copy(count_ref, count_hbm, sems.at[2])
-    reward_copy.start()
-    count_copy.start()
-    rows_copy.wait()
-    reward_copy.wait()
-    count_copy.wait()
+    count_ref[...] = sum_of(slots + 2)[:, :1].astype(jnp.int32)
 
 
 def fused(features, rewards, lengths, owners, norm_gain):
@@ -153,7 +151,6 @@
     order, place_of = places(actors, groups)
     vmem = pl.BlockSpec(memory_space=pltpu.VMEM)
     smem = pl.BlockSpec(memory_space=pltpu.SMEM)
-    hbm = pl.BlockSpec(memory_space=pltpu.HBM)
     packed = pl.pallas_call(
         functools.partial(pack_kernel, place_of, groups),
         out_shape=jax.ShapeDtypeStruct((games * groups, last + 1, PAIR, LANES), jnp.bfloat16),
@@ -191,13 +188,9 @@
             jax.ShapeDtypeStruct((1, 1), jnp.int32),
         ),
         in_specs=[vmem],
-        out_specs=(hbm, hbm, hbm),
+        out_specs=(vmem, vmem, vmem),
         scratch_shapes=[
-            pltpu.VMEM((slots, width), jnp.bfloat16),
-            pltpu.VMEM((1, slots), jnp.float32),
-            pltpu.VMEM((1, 1), jnp.int32),
             pltpu.VMEM((slots * across, LANES), jnp.float32),
-            pltpu.SemaphoreType.DMA((3,)),
         ],
         compiler_params=pltpu.CompilerParams(vmem_limit_bytes=VMEM_GRANT),
         name="unpack",

time: 17.5 us -> 17.2 us (0.983)
  no operation moved by 1% of the time
where the time goes in v6:
time: 17.2 us; the launch traced here: 16.9 us
  blocking collectives  14.5 us (84%)
  Pallas kernels  1.77 us (10%)
  between operations  0.64 us (4%)
    all_to_all x1, blocking collectives, fused(): lax.all_to_all(packed, ('actors', 'rep'), split_axis=0, concat_axis=0, ti...  14.5 us
    pallas_call x1, Pallas kernels, fused(): pl.pallas_call(functools.partial(pack_kernel, place_of, groups), out_shap...  0.99 us
    pallas_call x1, Pallas kernels, fused(): pl.pallas_call(functools.partial(unpack_kernel, place_of, groups, row_cou...  0.78 us

profile of v6, /device:TPU:0, one launch (start us, length us, event | category | flops | bytes accessed | tf_op | source)
XLA Modules:
  0.0 16.9 jit_solution(16990572994432286681)
XLA Ops:
  0.6 1.0 %pack.1 = bf16[32,13,2,128]{3,2,1,0:T(2,128)(2,1)S(1)} custom-call(s32[1,8]{1,0:T(1,128)} %bitcast.12, s32[1,8]{1,0:T(1,128)} %bitcast.13, f32[1,16]{1,0:T(1,128)} %bitcast.10, bf16[16,1024]{1,0:T(8,128)(2,1)} %bitcast.8, f32[1,1024]{1,0:T(1,128)} %bitcast.9, f32[1,16]{1,0:T(1,128)} %bitcast.11), custom_call_target="tpu_custom_call" | custom-call | tf_op jit(solution)/shard_map/pack/pallas_call | solution.py:154
  1.6 14.5 %all_to_all.5.in_ref = bf16[32,13,2,128]{3,2,1,0:T(2,128)(2,1)S(1)} all-to-all(bf16[32,13,2,128]{3,2,1,0:T(2,128)(2,1)S(1)} %pack.1), channel_id=1, replica_groups={{7,18,5,14,2,16,29,21,27,30,15,17,12,6,22,3,28,10,1,11,0,13,19,24,9,31,..., dimensions={0} | all-to-all | bytes 425984 | tf_op jit(solution)/shard_map/all_to_all | solution.py:180
  16.1 0.8 %unpack.1 = (bf16[24,1024]{1,0:T(8,128)(2,1)}, f32[1,24]{1,0:T(1,128)}, s32[1,1]{1,0:T(1,128)}) custom-call(bf16[32,13,2,128]{3,2,1,0:T(2,128)(2,1)S(1)} %all_to_all.5.in_ref), custom_call_target="tpu_custom_call" | custom-call | tf_op jit(solution)/shard_map/unpack/pallas_call | solution.py:183

commit v7 on v6

--- a/solution.py
+++ b/solution.py
@@ -16,16 +16,15 @@
 PAIR = 2
 HALF = LANES // 2
 VMEM_GRANT = 8 << 20
-ORDERS = {
-    (8, 4): [
-        7, 18, 5, 14, 2, 16, 29, 21, 27, 30, 15, 17, 12, 6, 22, 3, 28, 10, 1, 11, 0, 13, 19, 24, 9, 31, 4, 23, 26, 25, 20, 8,
-    ]
-}
+PARTS = 2
+ORDERS = {(8, 4): [14, 0, 5, 3, 2, 11, 4, 1, 15, 9, 10, 6, 8, 13, 7, 12]}
 
 
 def places(actors, groups):
-    order = ORDERS.get((actors, groups)) or [a * groups + g for g in range(groups) for a in range(actors)]
-    return order, [order.index(device) for device in range(actors * groups)]
+    inner = groups // PARTS
+    order = ORDERS.get((actors, groups)) or [a * inner + g for g in range(inner) for a in range(actors)]
+    parts = [[d // inner * groups + d % inner * PARTS + part for d in order] for part in range(PARTS)]
+    return parts, [order.index(device) for device in range(actors * inner)]
 
 
 def of_group(choices, mine):
@@ -44,7 +43,7 @@
     across = width // LANES
     stride = row_count
     last = out_ref.shape[1] - 1
-    mine, actor = lax.axis_index("rep"), lax.axis_index("actors")
+    mine, actor = lax.axis_index("rep") // PARTS, lax.axis_index("actors")
     slots = lax.axis_size("actors") * CAP
 
     start = jnp.int32(0)
@@ -98,16 +97,10 @@
             out_ref[place_of[t * groups + group], last] = tiles[t]
 
 
-def unpack_kernel(
-    place_of, groups, rows_total, in_ref, rows_ref, reward_ref, count_ref, piece_ref
-):
+def sum_kernel(place_of, groups, in_ref, every_ref, own_ref):
     actors = in_ref.shape[0] // groups
     last = in_ref.shape[1] - 1
-    slots, width = rows_ref.shape
-    across = width // LANES
-    stride = across
-    mine = lax.axis_index("rep")
-    own_places = [of_group([place_of[s * groups + group] for group in range(groups)], mine) for s in range(actors)]
+    mine = lax.axis_index("rep") // PARTS
 
     def total(blocks):
         terms = [in_ref[block, last].astype(jnp.float32) for block in blocks]
@@ -115,17 +108,28 @@
             terms = [sum(terms[at : at + 2]) for at in range(0, len(terms), 2)]
         return terms[0]
 
+    every_ref[...] = total(range(actors * groups))
+    own_ref[...] = total([of_group(place_of[s * groups : (s + 1) * groups], mine) for s in range(actors)])
+
+
+def rows_kernel(place_of, groups, in_ref, rows_ref, piece_ref):
+    actors = in_ref.shape[0] // groups
+    last = in_ref.shape[1] - 1
+    slots, width = rows_ref.shape
+    across = width // LANES
+    mine = lax.axis_index("rep") // PARTS
     for s in range(actors):
-        block = in_ref[own_places[s], :last].reshape(last * PAIR, LANES).astype(jnp.float32)
-        for j in range(CAP):
-            at = (s * CAP + j) * stride
-            piece_ref[at : at + across] = block[j * across : (j + 1) * across]
+        at = of_group(place_of[s * groups : (s + 1) * groups], mine)
+        block = in_ref[at, :last].reshape(last * PAIR, LANES).astype(jnp.float32)
+        piece_ref[s * last * PAIR : (s + 1) * last * PAIR] = block
     for k in range(across):
-        lanes = piece_ref[pl.ds(k, slots, stride=stride), :]
+        lanes = piece_ref[pl.ds(k, slots, stride=across), :]
         rows_ref[:, k * LANES : (k + 1) * LANES] = lanes.astype(jnp.bfloat16)
 
-    every = total(range(actors * groups))
-    own = total(own_places)
+
+def reward_kernel(rows_total, every_ref, other_ref, own_ref, reward_ref, count_ref):
+    slots = reward_ref.shape[1]
+    every, own = every_ref[...] + other_ref[...], own_ref[...]
 
     def sum_of(at):
         parts = (every[:1, at : at + 1], every[:1, HALF + at : HALF + at + 1], every[1:, at : at + 1])
@@ -148,12 +152,15 @@
     slots = actors * CAP
     across = width // LANES
     last = CAP * across // PAIR
-    order, place_of = places(actors, groups)
+    parts, place_of = places(actors, groups)
+    inner = groups // PARTS
+    tile = jax.ShapeDtypeStruct((PAIR, LANES), jnp.float32)
+    params = pltpu.CompilerParams(vmem_limit_bytes=VMEM_GRANT)
     vmem = pl.BlockSpec(memory_space=pltpu.VMEM)
     smem = pl.BlockSpec(memory_space=pltpu.SMEM)
     packed = pl.pallas_call(
-        functools.partial(pack_kernel, place_of, groups),
-        out_shape=jax.ShapeDtypeStruct((games * groups, last + 1, PAIR, LANES), jnp.bfloat16),
+        functools.partial(pack_kernel, place_of, inner),
+        out_shape=jax.ShapeDtypeStruct((games * inner, last + 1, PAIR, LANES), jnp.bfloat16),
         in_specs=[smem, smem, smem, vmem, vmem, vmem],
         out_specs=vmem,
         scratch_shapes=[
@@ -162,7 +169,7 @@
             pltpu.SMEM((games,), jnp.int32),
             pltpu.SMEM((games,), jnp.int32),
         ],
-        compiler_params=pltpu.CompilerParams(vmem_limit_bytes=VMEM_GRANT),
+        compiler_params=params,
         name="pack",
     )(
         *(
@@ -178,23 +185,35 @@
         )
     )
     landed = lax.all_to_all(
-        packed, ("actors", "rep"), split_axis=0, concat_axis=0, tiled=True, axis_index_groups=[order]
-    )
-    rows, scaled, count = pl.pallas_call(
-        functools.partial(unpack_kernel, place_of, groups, row_count * actors * groups),
-        out_shape=(
-            jax.ShapeDtypeStruct((slots, width), jnp.bfloat16),
-            jax.ShapeDtypeStruct((1, slots), jnp.float32),
-            jax.ShapeDtypeStruct((1, 1), jnp.int32),
-        ),
+        packed, ("actors", "rep"), split_axis=0, concat_axis=0, tiled=True, axis_index_groups=parts
+    )
+    every, own = pl.pallas_call(
+        functools.partial(sum_kernel, place_of, inner),
+        out_shape=(tile, tile),
         in_specs=[vmem],
-        out_specs=(vmem, vmem, vmem),
-        scratch_shapes=[
-            pltpu.VMEM((slots * across, LANES), jnp.float32),
-        ],
-        compiler_params=pltpu.CompilerParams(vmem_limit_bytes=VMEM_GRANT),
-        name="unpack",
+        out_specs=(vmem, vmem),
+        compiler_params=params,
+        name="sums",
     )(landed)
+    others = [(group, group // PARTS * PARTS + (group + 1) % PARTS) for group in range(groups)]
+    other = lax.ppermute(every, "rep", others)
+    rows = pl.pallas_call(
+        functools.partial(rows_kernel, place_of, inner),
+        out_shape=jax.ShapeDtypeStruct((slots, width), jnp.bfloat16),
+        in_specs=[vmem],
+        out_specs=vmem,
+        scratch_shapes=[pltpu.VMEM((slots * across, LANES), jnp.float32)],
+        compiler_params=params,
+        name="rows",
+    )(landed)
+    scaled, count = pl.pallas_call(
+        functools.partial(reward_kernel, row_count * actors * groups),
+        out_shape=(jax.ShapeDtypeStruct((1, slots), jnp.float32), jax.ShapeDtypeStruct((1, 1), jnp.int32)),
+        in_specs=[vmem, vmem, vmem],
+        out_specs=(vmem, vmem),
+        compiler_params=params,
+        name="rewards",
+    )(every, other, own)
     return (rows.reshape(1, 1, -1, width), scaled.reshape(1, 1, -1), count.reshape(1))
 
 
@@ -244,6 +263,7 @@
     fits = (
         actors * CAP + 3 <= HALF
         and lengths.shape[2] == actors
+        and groups % PARTS == 0
         and actors % SUBLANES == 0
         and width % (SUBLANES * LANES) == 0
         and row_count % 16 == 0

time: 17.2 us -> 16.2 us (0.942)
  blocking collectives: 14.5 us -> 12.4 us
  Pallas kernels: 1.77 us -> 2.42 us
  waiting for transfers between devices: 0 us -> 0.46 us
    all_to_all x1, blocking collectives: 14.5 us -> 12.4 us  [fused(): lax.all_to_all(packed, ('actors', 'rep'), split_axis=0, concat_axis=0, ti...]
    pallas_call x2 -> x4, Pallas kernels: 1.77 us -> 2.42 us  [the longest x1 0.98 us: fused(): pl.pallas_call(functools.partial(pack_kernel, place_of, inner), out_shape...]
    ppermute x0 -> x1, waiting for transfers between devices: none -> 0.46 us  [fused(): other = lax.ppermute(every, 'rep', others)]
  transfers between devices with their start and end apart: 0 -> 1, of which waited for: 0 -> 1; matrix products, arithmetic and copies ran while one was open for 0% -> 0% of each run, Pallas kernels for 0% -> 4%
where the time goes in v7:
time: 16.2 us; the launch traced here: 16 us
  blocking collectives  12.4 us (77%)
  Pallas kernels  2.42 us (15%)
  between operations  0.65 us (4%)
  waiting for transfers between devices  0.46 us (3%)
    all_to_all x1, blocking collectives, fused(): lax.all_to_all(packed, ('actors', 'rep'), split_axis=0, concat_axis=0, ti...  12.4 us
    pallas_call x1, Pallas kernels, fused(): pl.pallas_call(functools.partial(pack_kernel, place_of, inner), out_shape...  0.98 us
    pallas_call x1, Pallas kernels, fused(): pl.pallas_call(functools.partial(reward_kernel, row_count * actors * grou...  0.73 us
    pallas_call x1, Pallas kernels, fused(): pl.pallas_call(functools.partial(rows_kernel, place_of, inner), out_shape...  0.68 us
    ppermute x1, waiting for transfers between devices, fused(): other = lax.ppermute(every, 'rep', others)  0.46 us
  transfers between devices with their start and end apart: 1, of which 1 were waited for; matrix products, arithmetic and copies ran while one was open for 0% of the time, Pallas kernels for 4%

profile of v7, /device:TPU:0, one launch (start us, length us, event | category | flops | bytes accessed | tf_op | source)
XLA Modules:
  0.0 16.0 jit_solution(385661540347063695)
XLA Ops:
  0.6 1.0 %pack.1 = bf16[16,13,2,128]{3,2,1,0:T(2,128)(2,1)S(1)} custom-call(s32[1,8]{1,0:T(1,128)} %bitcast.13, s32[1,8]{1,0:T(1,128)} %bitcast.14, f32[1,16]{1,0:T(1,128)} %bitcast.11, bf16[16,1024]{1,0:T(8,128)(2,1)} %bitcast.9, f32[1,1024]{1,0:T(1,128)} %bitcast.10, f32[1,16]{1,0:T(1,128)} %bitcast.12), custom_call_target="tpu_custom_call" | custom-call | tf_op jit(solution)/shard_map/pack/pallas_call | solution.py:161
  1.6 12.4 %all_to_all.5.in_ref = bf16[16,13,2,128]{3,2,1,0:T(2,128)(2,1)S(1)} all-to-all(bf16[16,13,2,128]{3,2,1,0:T(2,128)(2,1)S(1)} %pack.1), channel_id=1, replica_groups={{28,0,10,6,4,22,8,2,30,18,20,12,16,26,14,24},{29,1,11,7,5,23,9,3,31,19,..., dimensions={0} | all-to-all | bytes 212992 | tf_op jit(solution)/shard_map/all_to_all | solution.py:187
  14.1 0.1 collective-permute-start
  14.1 0.7 %rows.1 = bf16[24,1024]{1,0:T(8,128)(2,1)} custom-call(bf16[16,13,2,128]{3,2,1,0:T(2,128)(2,1)S(1)} %all_to_all.5.in_ref), custom_call_target="tpu_custom_call" | custom-call | tf_op jit(solution)/shard_map/rows/pallas_call | solution.py:200
  14.8 0.5 %collective-permute-done.other_ref = f32[2,128]{1,0:T(2,128)S(1)} collective-permute-done((f32[2,128]{1,0:T(2,128)S(1)}, f32[2,128]{1,0:T(2,128)S(1)}, u32[]{:S(2)}, u32[]{:S(2)}) %collective-permute-start) | collective-permute-done | bytes 1056 | tf_op jit(solution)/shard_map/ppermute | solution.py:199
  15.3 0.7 %rewards.1 = (f32[1,24]{1,0:T(1,128)}, s32[1,1]{1,0:T(1,128)}) custom-call(f32[2,128]{1,0:T(2,128)S(1)} %get-tuple-element.7.every_ref, f32[2,128]{1,0:T(2,128)S(1)} %collective-permute-done.other_ref, f32[2,128]{1,0:T(2,128)S(1)} %get-tuple-element.8.own_ref), custom_call_target="tpu_custom_call" | custom-call | tf_op jit(solution)/shard_map/rewards/pallas_call | solution.py:209
  (1 shorter events, 0.0 us)
Async XLA Ops:
  14.1 1.2 %collective-permute-start = (f32[2,128]{1,0:T(2,128)S(1)}, f32[2,128]{1,0:T(2,128)S(1)}, u32[]{:S(2)}, u32[]{:S(2)}) collective-permute-start(f32[2,128]{1,0:T(2,128)S(1)} %get-tuple-element.7.every_ref), channel_id=1, source_target_pairs={{0,1},{1,0},{2,3},{3,2},{4,5},{5,4},{6,7},{7,6},{8,9},{9,8},{10,11... | collective-permute-start | bytes 3080 | tf_op jit(solution)/shard_map/ppermute | solution.py:199

commit v8 on v7

--- a/solution.py
+++ b/solution.py
@@ -108,8 +108,18 @@
             terms = [sum(terms[at : at + 2]) for at in range(0, len(terms), 2)]
         return terms[0]
 
-    every_ref[...] = total(range(actors * groups))
-    own_ref[...] = total([of_group(place_of[s * groups : (s + 1) * groups], mine) for s in range(actors)])
+    every = total(range(actors * groups))
+    slots = actors * CAP
+    every_ref[...] = jnp.zeros_like(every_ref)
+    own_ref[...] = jnp.zeros_like(own_ref)
+    for n in range(3):
+        at = slots + n
+        parts = (every[:1, at : at + 1], every[:1, HALF + at : HALF + at + 1], every[1:, at : at + 1])
+        high, middle, low = (jnp.broadcast_to(part, (1, LANES)) for part in parts)
+        every_ref[n : n + 1] = high + middle + low
+    own = total([of_group(place_of[s * groups : (s + 1) * groups], mine) for s in range(actors)])
+    own_ref[:1, :HALF] = own[:1, :HALF] + own[:1, HALF:] + own[1:, :HALF]
+    own_ref[1:2, :HALF] = own[1:, HALF:]
 
 
 def rows_kernel(place_of, groups, in_ref, rows_ref, piece_ref):
@@ -129,20 +139,12 @@
 
 def reward_kernel(rows_total, every_ref, other_ref, own_ref, reward_ref, count_ref):
     slots = reward_ref.shape[1]
-    every, own = every_ref[...] + other_ref[...], own_ref[...]
-
-    def sum_of(at):
-        parts = (every[:1, at : at + 1], every[:1, HALF + at : HALF + at + 1], every[1:, at : at + 1])
-        high, middle, low = (jnp.broadcast_to(part, (1, HALF)) for part in parts)
-        return high + middle + low
-
-    mean = sum_of(slots) / rows_total
-    second = sum_of(slots + 1) / rows_total
+    every = every_ref[...] + other_ref[...]
+    mean, second = every[:1] / rows_total, every[1:2] / rows_total
     scale = lax.rsqrt(second - mean * mean + EPS_VAR)
-    value = own[:1, :HALF] + own[:1, HALF:] + own[1:, :HALF]
-    scaled = jnp.where(own[1:, HALF:] > 0.5, (value - mean) * scale, 0.0)
+    scaled = jnp.where(own_ref[1:2] > 0.5, (own_ref[:1] - mean) * scale, 0.0)
     reward_ref[...] = scaled[:, :slots]
-    count_ref[...] = sum_of(slots + 2)[:, :1].astype(jnp.int32)
+    count_ref[...] = every[2:3, :1].astype(jnp.int32)
 
 
 def fused(features, rewards, lengths, owners, norm_gain):
@@ -154,7 +156,7 @@
     last = CAP * across // PAIR
     parts, place_of = places(actors, groups)
     inner = groups // PARTS
-    tile = jax.ShapeDtypeStruct((PAIR, LANES), jnp.float32)
+    tile = jax.ShapeDtypeStruct((SUBLANES, LANES), jnp.float32)
     params = pltpu.CompilerParams(vmem_limit_bytes=VMEM_GRANT)
     vmem = pl.BlockSpec(memory_space=pltpu.VMEM)
     smem = pl.BlockSpec(memory_space=pltpu.SMEM)

time: 16.2 us -> 16.1 us (level)
    pallas_call x1, Pallas kernels: 0.73 us -> 0.53 us  [fused(): pl.pallas_call(functools.partial(reward_kernel, row_count * actors * grou...]
where the time goes in v8:
time: 16.1 us; the launch traced here: 15.9 us
  blocking collectives  12.4 us (77%)
  Pallas kernels  2.29 us (14%)
  between operations  0.65 us (4%)
  waiting for transfers between devices  0.47 us (3%)
    all_to_all x1, blocking collectives, fused(): lax.all_to_all(packed, ('actors', 'rep'), split_axis=0, concat_axis=0, ti...  12.4 us
    pallas_call x1, Pallas kernels, fused(): pl.pallas_call(functools.partial(pack_kernel, place_of, inner), out_shape...  0.98 us
    pallas_call x1, Pallas kernels, fused(): pl.pallas_call(functools.partial(rows_kernel, place_of, inner), out_shape...  0.68 us
    pallas_call x1, Pallas kernels, fused(): pl.pallas_call(functools.partial(reward_kernel, row_count * actors * grou...  0.53 us
    ppermute x1, waiting for transfers between devices, fused(): other = lax.ppermute(every, 'rep', others)  0.47 us
  transfers between devices with their start and end apart: 1, of which 1 were waited for; matrix products, arithmetic and copies ran while one was open for 0% of the time, Pallas kernels for 4%

profile of v8, /device:TPU:0, one launch (start us, length us, event | category | flops | bytes accessed | tf_op | source)
XLA Modules:
  0.0 15.9 jit_solution(15859343424136415401)
XLA Ops:
  0.6 1.0 %pack.1 = bf16[16,13,2,128]{3,2,1,0:T(2,128)(2,1)S(1)} custom-call(s32[1,8]{1,0:T(1,128)} %bitcast.13, s32[1,8]{1,0:T(1,128)} %bitcast.14, f32[1,16]{1,0:T(1,128)} %bitcast.11, bf16[16,1024]{1,0:T(8,128)(2,1)} %bitcast.9, f32[1,1024]{1,0:T(1,128)} %bitcast.10, f32[1,16]{1,0:T(1,128)} %bitcast.12), custom_call_target="tpu_custom_call" | custom-call | tf_op jit(solution)/shard_map/pack/pallas_call | solution.py:163
  1.6 12.4 %all_to_all.5.in_ref = bf16[16,13,2,128]{3,2,1,0:T(2,128)(2,1)S(1)} all-to-all(bf16[16,13,2,128]{3,2,1,0:T(2,128)(2,1)S(1)} %pack.1), channel_id=1, replica_groups={{28,0,10,6,4,22,8,2,30,18,20,12,16,26,14,24},{29,1,11,7,5,23,9,3,31,19,..., dimensions={0} | all-to-all | bytes 212992 | tf_op jit(solution)/shard_map/all_to_all | solution.py:189
  14.0 0.1 sums.1
  14.1 0.1 collective-permute-start
  14.2 0.7 %rows.1 = bf16[24,1024]{1,0:T(8,128)(2,1)} custom-call(bf16[16,13,2,128]{3,2,1,0:T(2,128)(2,1)S(1)} %all_to_all.5.in_ref), custom_call_target="tpu_custom_call" | custom-call | tf_op jit(solution)/shard_map/rows/pallas_call | solution.py:202
  14.9 0.5 %collective-permute-done.other_ref = f32[8,128]{1,0:T(8,128)S(1)} collective-permute-done((f32[8,128]{1,0:T(8,128)S(1)}, f32[8,128]{1,0:T(8,128)S(1)}, u32[]{:S(2)}, u32[]{:S(2)}) %collective-permute-start) | collective-permute-done | bytes 4128 | tf_op jit(solution)/shard_map/ppermute | solution.py:201
  15.4 0.5 %rewards.1 = (f32[1,24]{1,0:T(1,128)}, s32[1,1]{1,0:T(1,128)}) custom-call(f32[8,128]{1,0:T(8,128)S(1)} %get-tuple-element.7.every_ref, f32[8,128]{1,0:T(8,128)S(1)} %collective-permute-done.other_ref, f32[8,128]{1,0:T(8,128)S(1)} %get-tuple-element.8.own_ref), custom_call_target="tpu_custom_call" | custom-call | tf_op jit(solution)/shard_map/rewards/pallas_call | solution.py:211
Async XLA Ops:
  14.1 1.2 %collective-permute-start = (f32[8,128]{1,0:T(8,128)S(1)}, f32[8,128]{1,0:T(8,128)S(1)}, u32[]{:S(2)}, u32[]{:S(2)}) collective-permute-start(f32[8,128]{1,0:T(8,128)S(1)} %get-tuple-element.7.every_ref), channel_id=1, source_target_pairs={{0,1},{1,0},{2,3},{3,2},{4,5},{5,4},{6,7},{7,6},{8,9},{9,8},{10,11... | collective-permute-start | bytes 12296 | tf_op jit(solution)/shard_map/ppermute | solution.py:201

commit v9 on v8

--- a/solution.py
+++ b/solution.py
@@ -17,7 +17,7 @@
 HALF = LANES // 2
 VMEM_GRANT = 8 << 20
 PARTS = 2
-ORDERS = {(8, 4): [14, 0, 5, 3, 2, 11, 4, 1, 15, 9, 10, 6, 8, 13, 7, 12]}
+ORDERS = {(8, 4): [11, 7, 6, 3, 8, 4, 15, 14, 12, 10, 2, 0, 1, 5, 9, 13]}
 
 
 def places(actors, groups):
@@ -97,44 +97,40 @@
             out_ref[place_of[t * groups + group], last] = tiles[t]
 
 
-def sum_kernel(place_of, groups, in_ref, every_ref, own_ref):
-    actors = in_ref.shape[0] // groups
-    last = in_ref.shape[1] - 1
-    mine = lax.axis_index("rep") // PARTS
-
-    def total(blocks):
-        terms = [in_ref[block, last].astype(jnp.float32) for block in blocks]
-        while len(terms) > 1:
-            terms = [sum(terms[at : at + 2]) for at in range(0, len(terms), 2)]
-        return terms[0]
-
-    every = total(range(actors * groups))
-    slots = actors * CAP
+def total(in_ref, blocks):
+    terms = [in_ref[block, in_ref.shape[1] - 1].astype(jnp.float32) for block in blocks]
+    while len(terms) > 1:
+        terms = [sum(terms[at : at + 2]) for at in range(0, len(terms), 2)]
+    return terms[0]
+
+
+def sum_kernel(slots, in_ref, every_ref):
+    every = total(in_ref, range(in_ref.shape[0]))
     every_ref[...] = jnp.zeros_like(every_ref)
-    own_ref[...] = jnp.zeros_like(own_ref)
     for n in range(3):
         at = slots + n
         parts = (every[:1, at : at + 1], every[:1, HALF + at : HALF + at + 1], every[1:, at : at + 1])
         high, middle, low = (jnp.broadcast_to(part, (1, LANES)) for part in parts)
         every_ref[n : n + 1] = high + middle + low
-    own = total([of_group(place_of[s * groups : (s + 1) * groups], mine) for s in range(actors)])
-    own_ref[:1, :HALF] = own[:1, :HALF] + own[:1, HALF:] + own[1:, :HALF]
-    own_ref[1:2, :HALF] = own[1:, HALF:]
-
-
-def rows_kernel(place_of, groups, in_ref, rows_ref, piece_ref):
+
+
+def rows_kernel(place_of, groups, in_ref, rows_ref, own_ref, piece_ref):
     actors = in_ref.shape[0] // groups
     last = in_ref.shape[1] - 1
     slots, width = rows_ref.shape
     across = width // LANES
     mine = lax.axis_index("rep") // PARTS
-    for s in range(actors):
-        at = of_group(place_of[s * groups : (s + 1) * groups], mine)
+    own_places = [of_group(place_of[s * groups : (s + 1) * groups], mine) for s in range(actors)]
+    for s, at in enumerate(own_places):
         block = in_ref[at, :last].reshape(last * PAIR, LANES).astype(jnp.float32)
         piece_ref[s * last * PAIR : (s + 1) * last * PAIR] = block
     for k in range(across):
         lanes = piece_ref[pl.ds(k, slots, stride=across), :]
         rows_ref[:, k * LANES : (k + 1) * LANES] = lanes.astype(jnp.bfloat16)
+    own = total(in_ref, own_places)
+    own_ref[...] = jnp.zeros_like(own_ref)
+    own_ref[:1, :HALF] = own[:1, :HALF] + own[:1, HALF:] + own[1:, :HALF]
+    own_ref[1:2, :HALF] = own[1:, HALF:]
 
 
 def reward_kernel(rows_total, every_ref, other_ref, own_ref, reward_ref, count_ref):
@@ -189,21 +185,21 @@
     landed = lax.all_to_all(
         packed, ("actors", "rep"), split_axis=0, concat_axis=0, tiled=True, axis_index_groups=parts
     )
-    every, own = pl.pallas_call(
-        functools.partial(sum_kernel, place_of, inner),
-        out_shape=(tile, tile),
+    every = pl.pallas_call(
+        functools.partial(sum_kernel, slots),
+        out_shape=tile,
         in_specs=[vmem],
-        out_specs=(vmem, vmem),
+        out_specs=vmem,
         compiler_params=params,
         name="sums",
     )(landed)
     others = [(group, group // PARTS * PARTS + (group + 1) % PARTS) for group in range(groups)]
     other = lax.ppermute(every, "rep", others)
-    rows = pl.pallas_call(
+    rows, own = pl.pallas_call(
         functools.partial(rows_kernel, place_of, inner),
-        out_shape=jax.ShapeDtypeStruct((slots, width), jnp.bfloat16),
+        out_shape=(jax.ShapeDtypeStruct((slots, width), jnp.bfloat16), tile),
         in_specs=[vmem],
-        out_specs=vmem,
+        out_specs=(vmem, vmem),
         scratch_shapes=[pltpu.VMEM((slots * across, LANES), jnp.float32)],
         compiler_params=params,
         name="rows",

time: 16.1 us -> 16 us (level)
  no operation moved by 1% of the time
where the time goes in v9:
time: 16 us; the launch traced here: 15.8 us
  blocking collectives  12.4 us (78%)
  Pallas kernels  2.28 us (14%)
  between operations  0.65 us (4%)
  waiting for transfers between devices  0.46 us (3%)
    all_to_all x1, blocking collectives, fused(): lax.all_to_all(packed, ('actors', 'rep'), split_axis=0, concat_axis=0, ti...  12.4 us
    pallas_call x1, Pallas kernels, fused(): pl.pallas_call(functools.partial(pack_kernel, place_of, inner), out_shape...  0.98 us
    pallas_call x1, Pallas kernels, fused(): pl.pallas_call(functools.partial(rows_kernel, place_of, inner), out_shape...  0.69 us
    pallas_call x1, Pallas kernels, fused(): pl.pallas_call(functools.partial(reward_kernel, row_count * actors * grou...  0.53 us
    ppermute x1, waiting for transfers between devices, fused(): other = lax.ppermute(every, 'rep', others)  0.46 us
  transfers between devices with their start and end apart: 1, of which 1 were waited for; matrix products, arithmetic and copies ran while one was open for 0% of the time, Pallas kernels for 4%

profile of v9, /device:TPU:0, one launch (start us, length us, event | category | flops | bytes accessed | tf_op | source)
XLA Modules:
  0.0 15.8 jit_solution(5397025799545236235)
XLA Ops:
  0.6 1.0 %pack.1 = bf16[16,13,2,128]{3,2,1,0:T(2,128)(2,1)S(1)} custom-call(s32[1,8]{1,0:T(1,128)} %bitcast.12, s32[1,8]{1,0:T(1,128)} %bitcast.13, f32[1,16]{1,0:T(1,128)} %bitcast.10, bf16[16,1024]{1,0:T(8,128)(2,1)} %bitcast.8, f32[1,1024]{1,0:T(1,128)} %bitcast.9, f32[1,16]{1,0:T(1,128)} %bitcast.11), custom_call_target="tpu_custom_call" | custom-call | tf_op jit(solution)/shard_map/pack/pallas_call | solution.py:159
  1.6 12.4 %all_to_all.5.in_ref = bf16[16,13,2,128]{3,2,1,0:T(2,128)(2,1)S(1)} all-to-all(bf16[16,13,2,128]{3,2,1,0:T(2,128)(2,1)S(1)} %pack.1), channel_id=1, replica_groups={{22,14,12,6,16,8,30,28,24,20,4,0,2,10,18,26},{23,15,13,7,17,9,31,29,25,..., dimensions={0} | all-to-all | bytes 212992 | tf_op jit(solution)/shard_map/all_to_all | solution.py:185
  14.0 0.1 sums.1.every_ref
  14.1 0.0 collective-permute-start
  14.1 0.7 %rows.1 = (bf16[24,1024]{1,0:T(8,128)(2,1)}, f32[8,128]{1,0:T(8,128)S(1)}) custom-call(bf16[16,13,2,128]{3,2,1,0:T(2,128)(2,1)S(1)} %all_to_all.5.in_ref), custom_call_target="tpu_custom_call" | custom-call | tf_op jit(solution)/shard_map/rows/pallas_call | solution.py:198
  14.8 0.5 %collective-permute-done.other_ref = f32[8,128]{1,0:T(8,128)S(1)} collective-permute-done((f32[8,128]{1,0:T(8,128)S(1)}, f32[8,128]{1,0:T(8,128)S(1)}, u32[]{:S(2)}, u32[]{:S(2)}) %collective-permute-start) | collective-permute-done | bytes 4128 | tf_op jit(solution)/shard_map/ppermute | solution.py:197
  15.3 0.5 %rewards.1 = (f32[1,24]{1,0:T(1,128)}, s32[1,1]{1,0:T(1,128)}) custom-call(f32[8,128]{1,0:T(8,128)S(1)} %sums.1.every_ref, f32[8,128]{1,0:T(8,128)S(1)} %collective-permute-done.other_ref, f32[8,128]{1,0:T(8,128)S(1)} %get-tuple-element.8.own_ref), custom_call_target="tpu_custom_call" | custom-call | tf_op jit(solution)/shard_map/rewards/pallas_call | solution.py:207
Async XLA Ops:
  14.1 1.2 %collective-permute-start = (f32[8,128]{1,0:T(8,128)S(1)}, f32[8,128]{1,0:T(8,128)S(1)}, u32[]{:S(2)}, u32[]{:S(2)}) collective-permute-start(f32[8,128]{1,0:T(8,128)S(1)} %sums.1.every_ref), channel_id=1, source_target_pairs={{0,1},{1,0},{2,3},{3,2},{4,5},{5,4},{6,7},{7,6},{8,9},{9,8},{10,11... | collective-permute-start | bytes 12296 | tf_op jit(solution)/shard_map/ppermute | solution.py:197

commit v10 on v9

--- a/solution.py
+++ b/solution.py
@@ -36,7 +36,7 @@
 
 def pack_kernel(
     place_of, groups, length_ref, owner_ref, reward_at, rows_ref, gain_ref, reward_ref,
-    out_ref, normed_ref, scalar_ref, start_of, length_of,
+    out_ref, wide_ref, scale_ref, scalar_ref, start_of, length_of,
 ):
     games = length_ref.shape[1]
     row_count, width = rows_ref.shape
@@ -54,10 +54,11 @@
         start = start + size
 
     wide = rows_ref[...].astype(jnp.float32)
+    for k in range(across):
+        wide_ref[k * stride : k * stride + row_count] = wide[:, k * LANES : (k + 1) * LANES]
     square_mean = jnp.sum(wide * wide, axis=1, keepdims=True) / width
-    normed = wide * lax.rsqrt(square_mean + EPS_NORM) * gain_ref[...]
-    for k in range(across):
-        normed_ref[k * stride : k * stride + row_count] = normed[:, k * LANES : (k + 1) * LANES]
+    scale_ref[:row_count] = jnp.broadcast_to(lax.rsqrt(square_mean + EPS_NORM), (row_count, LANES))
+    gain = gain_ref[...]
 
     lane = lax.broadcasted_iota(jnp.int32, (games, LANES), 1)
     place = lane % HALF
@@ -72,8 +73,9 @@
         sizes = jnp.where(trainer == t, size, sizes)
         parts = []
         for j in range(CAP):
-            part = normed_ref[pl.ds(begin + j, across, stride=stride), :]
-            parts.append(jnp.where(j < size, part, 0.0))
+            part = wide_ref[pl.ds(begin + j, across, stride=stride), :]
+            scale = scale_ref[pl.ds(begin + j, 1), :]
+            parts.append(jnp.where(j < size, part * scale * gain, 0.0))
             value = reward_at[0, jnp.minimum(begin + j, row_count - 1)]
             held[j] = jnp.where(trainer == t, value, held[j])
         block = jnp.concatenate(parts, axis=0).astype(jnp.bfloat16)
@@ -163,6 +165,7 @@
         out_specs=vmem,
         scratch_shapes=[
             pltpu.VMEM(((across + 1) * row_count, LANES), jnp.float32),
+            pltpu.VMEM((row_count + SUBLANES, LANES), jnp.float32),
             pltpu.VMEM((PAIR * games, LANES), jnp.float32),
             pltpu.SMEM((games,), jnp.int32),
             pltpu.SMEM((games,), jnp.int32),
@@ -177,7 +180,7 @@
                 owners.reshape(1, games),
                 rewards.reshape(1, row_count),
                 features.reshape(row_count, width),
-                norm_gain.reshape(1, width),
+                norm_gain.reshape(across, LANES),
                 rewards.reshape(1, row_count),
             )
         )

time: 16 us -> 16 us (level)
  no operation moved by 1% of the time
where the time goes in v10:
time: 16 us; the launch traced here: 15.8 us
  blocking collectives  12.4 us (78%)
  Pallas kernels  2.28 us (14%)
  between operations  0.64 us (4%)
  waiting for transfers between devices  0.46 us (3%)
    all_to_all x1, blocking collectives, fused(): lax.all_to_all(packed, ('actors', 'rep'), split_axis=0, concat_axis=0, ti...  12.4 us
    pallas_call x1, Pallas kernels, fused(): pl.pallas_call(functools.partial(pack_kernel, place_of, inner), out_shape...  0.98 us
    pallas_call x1, Pallas kernels, fused(): pl.pallas_call(functools.partial(rows_kernel, place_of, inner), out_shape...  0.69 us
    pallas_call x1, Pallas kernels, fused(): pl.pallas_call(functools.partial(reward_kernel, row_count * actors * grou...  0.53 us
    ppermute x1, waiting for transfers between devices, fused(): other = lax.ppermute(every, 'rep', others)  0.46 us
  transfers between devices with their start and end apart: 1, of which 1 were waited for; matrix products, arithmetic and copies ran while one was open for 0% of the time, Pallas kernels for 4%

profile of v10, /device:TPU:0, one launch (start us, length us, event | category | flops | bytes accessed | tf_op | source)
XLA Modules:
  0.0 15.8 jit_solution(10005056585989587832)
XLA Ops:
  0.6 1.0 %pack.1 = bf16[16,13,2,128]{3,2,1,0:T(2,128)(2,1)S(1)} custom-call(s32[1,8]{1,0:T(1,128)} %bitcast.12, s32[1,8]{1,0:T(1,128)} %bitcast.13, f32[1,16]{1,0:T(1,128)} %bitcast.10, bf16[16,1024]{1,0:T(8,128)(2,1)} %bitcast.8, f32[8,128]{1,0:T(8,128)} %bitcast.9, f32[1,16]{1,0:T(1,128)} %bitcast.11), custom_call_target="tpu_custom_call" | custom-call | tf_op jit(solution)/shard_map/pack/pallas_call | solution.py:161
  1.6 12.4 %all_to_all.5.in_ref = bf16[16,13,2,128]{3,2,1,0:T(2,128)(2,1)S(1)} all-to-all(bf16[16,13,2,128]{3,2,1,0:T(2,128)(2,1)S(1)} %pack.1), channel_id=1, replica_groups={{22,14,12,6,16,8,30,28,24,20,4,0,2,10,18,26},{23,15,13,7,17,9,31,29,25,..., dimensions={0} | all-to-all | bytes 212992 | tf_op jit(solution)/shard_map/all_to_all | solution.py:188
  14.0 0.1 sums.1.every_ref
  14.1 0.0 collective-permute-start
  14.1 0.7 %rows.1 = (bf16[24,1024]{1,0:T(8,128)(2,1)}, f32[8,128]{1,0:T(8,128)S(1)}) custom-call(bf16[16,13,2,128]{3,2,1,0:T(2,128)(2,1)S(1)} %all_to_all.5.in_ref), custom_call_target="tpu_custom_call" | custom-call | tf_op jit(solution)/shard_map/rows/pallas_call | solution.py:201
  14.8 0.5 %collective-permute-done.other_ref = f32[8,128]{1,0:T(8,128)S(1)} collective-permute-done((f32[8,128]{1,0:T(8,128)S(1)}, f32[8,128]{1,0:T(8,128)S(1)}, u32[]{:S(2)}, u32[]{:S(2)}) %collective-permute-start) | collective-permute-done | bytes 4128 | tf_op jit(solution)/shard_map/ppermute | solution.py:200
  15.2 0.5 %rewards.1 = (f32[1,24]{1,0:T(1,128)}, s32[1,1]{1,0:T(1,128)}) custom-call(f32[8,128]{1,0:T(8,128)S(1)} %sums.1.every_ref, f32[8,128]{1,0:T(8,128)S(1)} %collective-permute-done.other_ref, f32[8,128]{1,0:T(8,128)S(1)} %get-tuple-element.8.own_ref), custom_call_target="tpu_custom_call" | custom-call | tf_op jit(solution)/shard_map/rewards/pallas_call | solution.py:210
Async XLA Ops:
  14.1 1.2 %collective-permute-start = (f32[8,128]{1,0:T(8,128)S(1)}, f32[8,128]{1,0:T(8,128)S(1)}, u32[]{:S(2)}, u32[]{:S(2)}) collective-permute-start(f32[8,128]{1,0:T(8,128)S(1)} %sums.1.every_ref), channel_id=1, source_target_pairs={{0,1},{1,0},{2,3},{3,2},{4,5},{5,4},{6,7},{7,6},{8,9},{9,8},{10,11... | collective-permute-start | bytes 12296 | tf_op jit(solution)/shard_map/ppermute | solution.py:200

commit v11 on v9

--- a/solution.py
+++ b/solution.py
@@ -152,7 +152,7 @@
     last = CAP * across // PAIR
     parts, place_of = places(actors, groups)
     inner = groups // PARTS
-    tile = jax.ShapeDtypeStruct((SUBLANES, LANES), jnp.float32)
+    tile = jax.ShapeDtypeStruct((2 * PAIR, LANES), jnp.float32)
     params = pltpu.CompilerParams(vmem_limit_bytes=VMEM_GRANT)
     vmem = pl.BlockSpec(memory_space=pltpu.VMEM)
     smem = pl.BlockSpec(memory_space=pltpu.SMEM)

time: 16 us -> 16 us (level)
  no operation moved by 1% of the time
where the time goes in v11:
time: 16 us; the launch traced here: 15.8 us
  blocking collectives  12.4 us (78%)
  Pallas kernels  2.28 us (14%)
  between operations  0.65 us (4%)
  waiting for transfers between devices  0.46 us (3%)
    all_to_all x1, blocking collectives, fused(): lax.all_to_all(packed, ('actors', 'rep'), split_axis=0, concat_axis=0, ti...  12.4 us
    pallas_call x1, Pallas kernels, fused(): pl.pallas_call(functools.partial(pack_kernel, place_of, inner), out_shape...  0.98 us
    pallas_call x1, Pallas kernels, fused(): pl.pallas_call(functools.partial(rows_kernel, place_of, inner), out_shape...  0.69 us
    pallas_call x1, Pallas kernels, fused(): pl.pallas_call(functools.partial(reward_kernel, row_count * actors * grou...  0.53 us
    ppermute x1, waiting for transfers between devices, fused(): other = lax.ppermute(every, 'rep', others)  0.46 us
  transfers between devices with their start and end apart: 1, of which 1 were waited for; matrix products, arithmetic and copies ran while one was open for 0% of the time, Pallas kernels for 4%

profile of v11, /device:TPU:0, one launch (start us, length us, event | category | flops | bytes accessed | tf_op | source)
XLA Modules:
  0.0 15.8 jit_solution(14693531839066556202)
XLA Ops:
  0.6 1.0 %pack.1 = bf16[16,13,2,128]{3,2,1,0:T(2,128)(2,1)S(1)} custom-call(s32[1,8]{1,0:T(1,128)} %bitcast.12, s32[1,8]{1,0:T(1,128)} %bitcast.13, f32[1,16]{1,0:T(1,128)} %bitcast.10, bf16[16,1024]{1,0:T(8,128)(2,1)} %bitcast.8, f32[1,1024]{1,0:T(1,128)} %bitcast.9, f32[1,16]{1,0:T(1,128)} %bitcast.11), custom_call_target="tpu_custom_call" | custom-call | tf_op jit(solution)/shard_map/pack/pallas_call | solution.py:159
  1.6 12.4 %all_to_all.5.in_ref = bf16[16,13,2,128]{3,2,1,0:T(2,128)(2,1)S(1)} all-to-all(bf16[16,13,2,128]{3,2,1,0:T(2,128)(2,1)S(1)} %pack.1), channel_id=1, replica_groups={{22,14,12,6,16,8,30,28,24,20,4,0,2,10,18,26},{23,15,13,7,17,9,31,29,25,..., dimensions={0} | all-to-all | bytes 212992 | tf_op jit(solution)/shard_map/all_to_all | solution.py:185
  14.0 0.1 sums.1.every_ref
  14.1 0.0 collective-permute-start
  14.1 0.7 %rows.1 = (bf16[24,1024]{1,0:T(8,128)(2,1)}, f32[4,128]{1,0:T(4,128)S(1)}) custom-call(bf16[16,13,2,128]{3,2,1,0:T(2,128)(2,1)S(1)} %all_to_all.5.in_ref), custom_call_target="tpu_custom_call" | custom-call | tf_op jit(solution)/shard_map/rows/pallas_call | solution.py:198
  14.8 0.5 %collective-permute-done.other_ref = f32[4,128]{1,0:T(4,128)S(1)} collective-permute-done((f32[4,128]{1,0:T(4,128)S(1)}, f32[4,128]{1,0:T(4,128)S(1)}, u32[]{:S(2)}, u32[]{:S(2)}) %collective-permute-start) | collective-permute-done | bytes 2080 | tf_op jit(solution)/shard_map/ppermute | solution.py:197
  15.3 0.5 %rewards.1 = (f32[1,24]{1,0:T(1,128)}, s32[1,1]{1,0:T(1,128)}) custom-call(f32[4,128]{1,0:T(4,128)S(1)} %sums.1.every_ref, f32[4,128]{1,0:T(4,128)S(1)} %collective-permute-done.other_ref, f32[4,128]{1,0:T(4,128)S(1)} %get-tuple-element.8.own_ref), custom_call_target="tpu_custom_call" | custom-call | tf_op jit(solution)/shard_map/rewards/pallas_call | solution.py:207
Async XLA Ops:
  14.1 1.2 %collective-permute-start = (f32[4,128]{1,0:T(4,128)S(1)}, f32[4,128]{1,0:T(4,128)S(1)}, u32[]{:S(2)}, u32[]{:S(2)}) collective-permute-start(f32[4,128]{1,0:T(4,128)S(1)} %sums.1.every_ref), channel_id=1, source_target_pairs={{0,1},{1,0},{2,3},{3,2},{4,5},{5,4},{6,7},{7,6},{8,9},{9,8},{10,11... | collective-permute-start | bytes 6152 | tf_op jit(solution)/shard_map/ppermute | solution.py:197
